TPU v7x, 32 devices: a whole 2x2x4 slice. The times are simulated.
32 devices in a mesh: groups: 2 (over y), seq: 4 (over z), head: 2 (over x), sub: 2 (over core).
Axes of the slice: x: 2, y: 2, z: 4, core: 2. Of those that a mesh axis runs over, the one named last changes fastest.
Arguments:
- queries: bfloat16 [128, 128, 16, 128], P(('groups', 'seq'), None, ('head', 'sub')), parts along dimension 0, may hold values from -6 to 6
- keys: bfloat16 [128, 128, 16, 128], P(('groups', 'seq'), None, ('head', 'sub')), parts along dimension 0, may hold values from -6 to 6
- values: bfloat16 [128, 128, 16, 2, 128], P(('groups', 'seq'), None, ('head', 'sub')), parts along dimension 0, may hold values from -6 to 6
- log_decay: bfloat16 [128, 128, 16, 2], P(('groups', 'seq'), None, ('head', 'sub')), parts along dimension 0, may hold values from -0.8 to 0
- write_rate: bfloat16 [128, 128, 16, 2], P(('groups', 'seq'), None, ('head', 'sub')), parts along dimension 0, may hold values from 0.049804688 to 0.94921875
- norm_gain: bfloat16 [128], replicated, may hold values from 0.25 to 1.75
- parent_cache: float32 [32, 16, 2, 128, 128], P(('groups', 'seq'), ('head', 'sub')), parts along dimension 0, may hold values from -3 to 3
- order: int32 [128], P('groups'), parts along dimension 0, may hold values from 0 to 63, as said below
- parent_owner: int32 [128], P('groups'), parts along dimension 0, may hold values from 0 to 3, as said below
- parent_slot: int32 [128], P('groups'), parts along dimension 0, may hold values from 0 to 3
- token_count: int32 [128], P('groups'), parts along dimension 0, may hold values from 64 to 128, as said below
Outputs:
- mixed: bfloat16 [128, 128, 16, 2, 128], P(('groups', 'seq'), None, ('head', 'sub')), parts along dimension 0
- final_state: float32 [128, 16, 2, 128, 128], P(('groups', 'seq'), ('head', 'sub')), parts along dimension 0
There are 2 independent parts, one for each index of `groups`. A program takes and returns all parts, laid end to end along the dimension named above; an argument that names none is the same for every part. Nothing has to cross between parts.
Inputs may be any that keep to these rules, and one draw needn't show every extreme that they name: A permutation; slot j = p * 16 + s * 4 + r with r < 4 is processed by seq device p and holds an expansion that arrives on seq device s, so order[j] // 16 = s. `parent_owner`: among the 16 expansions processed by one seq device at most 8 have their parent on one owner, and on some device exactly 8 do. `token_count`: multiples of 64; some expansion has 128 and some has 64.
All inputs are finite; a program needn't handle non-finite values.
Results may differ from a plain program's by a relative error of at most 0.001.
Values may be sent and summed in bfloat16 or wider, within the bound.
A program may use at most 192 MiB of HBM per device.

v0:
```python
import functools

import jax
import jax.numpy as jnp
from jax import lax
from jax.experimental import pallas as pl
from jax.experimental.pallas import tpu as pltpu
from jax.sharding import PartitionSpec as P

norm_epsilon = 1e-06
BASE = 16
F32 = jnp.float32
BF16 = jnp.bfloat16
VMEM_BYTES = 56 * 1024 * 1024


def split(x):
    high = x.astype(BF16)
    low = (x - high.astype(F32)).astype(BF16)
    return high, low


def dot(a, b):
    return jnp.dot(a, b, preferred_element_type=F32)


def dot_nt(a, b):
    return lax.dot_general(a, b, (((1,), (1,)), ((), ())), preferred_element_type=F32)


def dot_tn(a, b):
    return lax.dot_general(a, b, (((0,), (0,)), ((), ())), preferred_element_type=F32)


def dot3(a, b):
    a_high, a_low = split(a)
    b_high, b_low = split(b)
    return dot3_split(a_high, a_low, b_high, b_low)


def dot3_split(a_high, a_low, b_high, b_low):
    return dot(a_high, b_high) + dot(a_low, b_high) + dot(a_high, b_low)


def prepare_kernel(count_ref, q_ref, k_ref, g_ref, b_ref, t_ref, m_ref, aux_ref,
                   q_rows, k_rows, a_rows):
    number = pl.program_id(0)
    live = count_ref[number]
    length, value_heads = g_ref.shape[1:]
    key_heads = value_heads // 2
    q_rows[...] = q_ref[0].astype(F32)
    k_rows[...] = k_ref[0].astype(F32)
    tokens = lax.broadcasted_iota(jnp.int32, (length, value_heads), 0)
    g = jnp.where(tokens < live, g_ref[0].astype(F32), 0.0)
    b = jnp.where(tokens < live, b_ref[0].astype(F32), 0.0)
    row = lax.broadcasted_iota(jnp.int32, (length, length), 0)
    col = lax.broadcasted_iota(jnp.int32, (length, length), 1)
    inclusive = row >= col
    strict = row > col
    diagonal = row == col
    ones_low = inclusive.astype(F32).astype(BF16)
    ones_up = (row <= col).astype(F32).astype(BF16)
    g_narrow = g.astype(BF16)
    g_col = dot(ones_low, g_narrow)
    g_row = dot_tn(g_narrow, ones_up)
    lane = lax.broadcasted_iota(jnp.int32, (BASE, length), 1)
    sub = lax.broadcasted_iota(jnp.int32, (BASE, length), 0)
    parts = length // BASE
    unit_cols = []
    compact = []
    for m in range(key_heads):
        q = q_rows[pl.ds(m, length, stride=key_heads), :].astype(BF16)
        k = k_rows[pl.ds(m, length, stride=key_heads), :].astype(BF16)
        both = dot_nt(jnp.concatenate([k, q], axis=0), k)
        kk = both[:length]
        qk = both[length:]
        squares = jnp.where(diagonal, kk, 0.0)
        n_row = lax.rsqrt(jnp.sum(squares, axis=0, keepdims=True) + norm_epsilon)
        n_col = lax.rsqrt(jnp.sum(squares, axis=1, keepdims=True) + norm_epsilon)
        unit_cols += [n_col, n_col]
        kk = kk * n_row * n_col
        qk = qk * n_row
        for r in range(2):
            h = 2 * m + r
            decay = jnp.exp(jnp.where(inclusive, g_col[:, h:h + 1] - g_row[h:h + 1, :], 0.0))
            m_ref[0, h] = jnp.where(inclusive, qk * decay, 0.0)
            a = jnp.where(strict, kk * decay * b[:, h:h + 1], 0.0)
            a_rows[h] = a
            piece = jnp.zeros((BASE, length), F32)
            for p in range(parts):
                piece = jnp.where(lane // BASE == p, a[p * BASE:(p + 1) * BASE], piece)
            compact.append(piece)
    inverses = [(lane % BASE == sub).astype(F32) for _ in range(value_heads)]
    for j in range(BASE - 1):
        index = (lane // BASE) * BASE + j
        for h in range(value_heads):
            factor = jnp.take_along_axis(compact[h], index, axis=1)
            inverses[h] = inverses[h] - factor * inverses[h][j:j + 1, :]
    for h in range(value_heads):
        a = a_rows[h]
        result = jnp.concatenate(
            [jnp.where(lane // BASE == p, inverses[h], 0.0) for p in range(parts)], axis=0
        )
        size = BASE
        while size < length:
            joined = (row // (2 * size) == col // (2 * size)) & (row // size != col // size)
            cross = jnp.where(joined, a, 0.0)
            result_high, result_low = split(result)
            cross_high, cross_low = split(cross)
            step = dot3_split(cross_high, cross_low, result_high, result_low)
            step_high, step_low = split(step)
            result = result - dot3_split(result_high, result_low, step_high, step_low)
            size *= 2
        t_ref[0, h] = result
    units = jnp.concatenate(unit_cols, axis=1)
    growth = jnp.exp(g_col)
    rest = jnp.exp(g_col[length - 1:length, :] - g_col) * units
    aux_ref[0] = jnp.concatenate([growth, b, b * growth * units, rest], axis=1)


def advance_kernel(ids_ref, parents_ref, count_ref, q_ref, k_ref, v_ref, t_ref, m_ref, aux_ref,
                   gain_ref, s_ref, old_ref, mixed_ref, state_ref,
                   q_rows, k_rows, v_rows, o_rows):
    del parents_ref, old_ref
    number = ids_ref[pl.program_id(0)]
    live = count_ref[number]
    value_heads, length = t_ref.shape[1:3]
    key_heads = value_heads // 2
    width = s_ref.shape[-1]
    q_rows[...] = q_ref[0].astype(F32)
    k_rows[...] = k_ref[0].astype(F32)
    v_rows[...] = v_ref[0].astype(F32)
    aux = aux_ref[0]
    gain = gain_ref[...].astype(F32)
    alive = lax.broadcasted_iota(jnp.int32, (length, width), 0) < live
    for m in range(key_heads):
        q = q_rows[pl.ds(m, length, stride=key_heads), :].astype(BF16)
        k = k_rows[pl.ds(m, length, stride=key_heads), :].astype(BF16)
        s = jnp.concatenate([s_ref[0, 2 * m], s_ref[0, 2 * m + 1]], axis=1)
        s_high, s_low = split(s)
        kq = jnp.concatenate([k, q], axis=0)
        applied = dot(jnp.concatenate([kq, kq], axis=1), jnp.concatenate([s_high, s_low], axis=0))
        updates = []
        for r in range(2):
            h = 2 * m + r
            growth = aux[:, h:h + 1]
            rate = aux[:, value_heads + h:value_heads + h + 1]
            scale = aux[:, 2 * value_heads + h:2 * value_heads + h + 1]
            rest = aux[:, 3 * value_heads + h:3 * value_heads + h + 1]
            v = v_rows[pl.ds(h, length, stride=value_heads), :]
            right = rate * v - scale * applied[:length, r * width:(r + 1) * width]
            fixed = dot3(t_ref[0, h], right)
            out = growth * applied[length:, r * width:(r + 1) * width] + dot3(m_ref[0, h], fixed)
            mean_square = jnp.mean(out * out, axis=1, keepdims=True)
            normed = out * lax.rsqrt(mean_square + norm_epsilon) * gain
            o_rows[pl.ds(h, length, stride=value_heads), :] = jnp.where(alive, normed, 0.0)
            updates.append(rest * fixed)
        update = jnp.concatenate(updates, axis=1)
        u_high, u_low = split(update)
        added = dot_tn(jnp.concatenate([k, k], axis=0), jnp.concatenate([u_high, u_low], axis=0))
        for r in range(2):
            h = 2 * m + r
            last = aux[length - 1:length, h:h + 1]
            state_ref[0, h] = last * s_ref[0, h] + added[:, r * width:(r + 1) * width]
    mixed_ref[0] = o_rows[...].astype(BF16)


def prepare(counts, queries, keys, decay, rate):
    expansions, length, value_heads = decay.shape
    rows, key_dim = queries.shape[1:]
    square = (expansions, value_heads, length, length)
    block = lambda shape: pl.BlockSpec((1,) + shape, lambda i, c: (i,) + (0,) * len(shape))
    work = expansions * value_heads
    return pl.pallas_call(
        prepare_kernel,
        out_shape=(
            jax.ShapeDtypeStruct(square, F32),
            jax.ShapeDtypeStruct(square, F32),
            jax.ShapeDtypeStruct((expansions, length, 4 * value_heads), F32),
        ),
        grid_spec=pltpu.PrefetchScalarGridSpec(
            num_scalar_prefetch=1,
            grid=(expansions,),
            in_specs=[
                block((rows, key_dim)),
                block((rows, key_dim)),
                block((length, value_heads)),
                block((length, value_heads)),
            ],
            out_specs=(
                block(square[1:]),
                block(square[1:]),
                block((length, 4 * value_heads)),
            ),
            scratch_shapes=[
                pltpu.VMEM((rows, key_dim), F32),
                pltpu.VMEM((rows, key_dim), F32),
                pltpu.VMEM((value_heads, length, length), F32),
            ],
        ),
        compiler_params=pltpu.CompilerParams(vmem_limit_bytes=VMEM_BYTES),
        cost_estimate=pl.CostEstimate(
            flops=work * 30 * 2 * length**3,
            bytes_accessed=work * 2 * 4 * length * length,
            transcendentals=work * length * length,
        ),
        name="prepare",
    )(counts, queries, keys, decay, rate)


def advance(ids, parents, counts, queries, keys, values, inverse, mixing, aux, gain, states, mixed):
    steps = ids.shape[0]
    value_heads, length = inverse.shape[1:3]
    rows, key_dim = queries.shape[1:]
    width = states.shape[-1]
    own = lambda shape: pl.BlockSpec(
        (1,) + shape, lambda i, ids, par, c: (ids[i],) + (0,) * len(shape)
    )
    state_block = (1, value_heads, key_dim, width)
    work = steps * value_heads
    return pl.pallas_call(
        advance_kernel,
        out_shape=(
            jax.ShapeDtypeStruct(mixed.shape, mixed.dtype),
            jax.ShapeDtypeStruct((steps,) + state_block[1:], F32),
        ),
        grid_spec=pltpu.PrefetchScalarGridSpec(
            num_scalar_prefetch=3,
            grid=(steps,),
            in_specs=[
                own((rows, key_dim)),
                own((rows, key_dim)),
                own((length * value_heads, width)),
                own((value_heads, length, length)),
                own((value_heads, length, length)),
                own((length, 4 * value_heads)),
                pl.BlockSpec((1, width), lambda i, ids, par, c: (0, 0)),
                pl.BlockSpec(state_block, lambda i, ids, par, c: (par[i], 0, 0, 0)),
                pl.BlockSpec(memory_space=pl.ANY),
            ],
            out_specs=(
                own((length * value_heads, width)),
                pl.BlockSpec(state_block, lambda i, ids, par, c: (i, 0, 0, 0)),
            ),
            scratch_shapes=[
                pltpu.VMEM((rows, key_dim), F32),
                pltpu.VMEM((rows, key_dim), F32),
                pltpu.VMEM((length * value_heads, width), F32),
                pltpu.VMEM((length * value_heads, width), F32),
            ],
        ),
        input_output_aliases={11: 0},
        compiler_params=pltpu.CompilerParams(vmem_limit_bytes=VMEM_BYTES),
        cost_estimate=pl.CostEstimate(
            flops=work * 12 * 2 * length**3,
            bytes_accessed=work * 5 * 4 * length * length,
            transcendentals=work * length,
        ),
        name="advance",
    )(ids, parents, counts, queries, keys, values, inverse, mixing, aux, gain, states, mixed)


def shards(queries, keys, values, log_decay, write_rate, norm_gain, parent_cache, order,
           parent_owner, parent_slot, token_count):
    seq_count = lax.axis_size("seq")
    me = lax.axis_index("seq")
    expansions, length, key_heads, key_dim = queries.shape
    value_heads = 2 * key_heads
    width = values.shape[-1]
    per_peer = expansions // seq_count
    cache_rows = parent_cache.shape[0]
    states = parent_cache.reshape(cache_rows, value_heads, key_dim, width)
    states = lax.all_gather(states, "seq", axis=0, tiled=True)
    start = me * expansions
    own = lambda table: lax.dynamic_slice_in_dim(table, start, expansions)
    counts = own(token_count)
    parents = own(parent_owner) * cache_rows + own(parent_slot)
    sends = lax.dynamic_slice_in_dim(
        order.reshape(seq_count, expansions), me * per_peer, per_peer, 1
    ) - start
    q = queries.reshape(expansions, length * key_heads, key_dim)
    k = keys.reshape(expansions, length * key_heads, key_dim)
    v = values.reshape(expansions, length * value_heads, width)
    decay = log_decay.reshape(expansions, length, value_heads)
    rate = write_rate.reshape(expansions, length, value_heads)
    inverse, mixing, aux = prepare(counts, q, k, decay, rate)
    mixed = jnp.zeros((expansions, length * value_heads, width), BF16)
    gain = norm_gain.reshape(1, width)
    final = jnp.zeros((expansions, value_heads, key_dim, width), F32)
    shifts = sorted(range(seq_count), key=lambda s: -min(s, seq_count - s))
    for shift in shifts:
        target = lax.rem(me + shift, seq_count)
        ids = lax.dynamic_index_in_dim(sends, target, 0, keepdims=False)
        mixed, chunk = advance(ids, jnp.take(parents, ids), counts, q, k, v, inverse, mixing, aux,
                               gain, states, mixed)
        if shift:
            chunk = lax.ppermute(
                chunk, "seq", [(d, (d + shift) % seq_count) for d in range(seq_count)]
            )
        source = lax.rem(me + seq_count - shift, seq_count)
        final = lax.dynamic_update_slice_in_dim(final, chunk, source * per_peer, 0)
    return (
        mixed.reshape(values.shape),
        final.reshape((expansions,) + parent_cache.shape[1:]),
    )


def solution(mesh):
    heads = ("head", "sub")
    rows = ("groups", "seq")
    placed = (
        P(rows, None, heads, None),
        P(rows, None, heads, None),
        P(rows, None, heads, None, None),
        P(rows, None, heads, None),
        P(rows, None, heads, None),
        P(),
        P(rows, heads, None, None, None),
        P("groups"),
        P("groups"),
        P("groups"),
        P("groups"),
    )
    return jax.shard_map(
        shards,
        mesh=mesh,
        in_specs=placed,
        out_specs=(P(rows, None, heads, None, None), P(rows, heads, None, None, None)),
        check_vma=False,
    )
```

profile of v0, /device:TPU:11, one launch (start us, length us, event | category | flops | bytes accessed | tf_op | source)
XLA Modules:
  0.0 368.8 jit_solution(12273098225453225196)
XLA Ops:
  7.2 0.0 all-gather.2.cloned.1.call-start
  7.2 0.7 all-gather.2.cloned.1.call-update
  7.9 0.7 reshape.39
  8.7 0.7 dynamic-slice_add_fusion
  9.4 0.1 fusion
  9.6 0.6 gather_fusion.1
  10.2 0.6 gather_fusion
  10.8 1.3 dynamic_slice.29.count_ref
  12.1 1.8 copy.25.g_ref
  13.9 1.8 copy.26.b_ref
  15.6 0.6 gather_fusion.3
  16.3 0.6 gather_fusion.2
  16.9 0.6 and_select_fusion
  17.5 110.4 %prepare.1 = (f32[16,8,128,128]{3,2,1,0:T(8,128)}, f32[16,8,128,128]{3,2,1,0:T(8,128)}, f32[16,128,32]{2,1,0:T(8,128)}) custom-call(s32[16]{0:T(128)} %dynamic_slice.29.count_ref, bf16[16,512,128]{2,1,0:T(8,128)(2,1)} %bitcast.26, bf16[16,512,128]{2,1,0:T(8,128)(2,1)} %bitcast.31, bf16[16,128,8]{2,1,0:T(8,128)(2,1)} %copy.25.g_ref, ...), custom_call_target="tpu_custom_call" | custom-call | flops 16106127360 | bytes 16777216 | tf_op jit(solution)/shard_map/prepare/pallas_call | solution.py:174
  127.9 29.7 %all-gather.2.cloned.1.call-done.s_ref = f32[16,8,128,128]{3,2,1,0:T(8,128)} async-done(((f32[4,8,128,128]{3,2,1,0:T(8,128)}), f32[16,8,128,128]{3,2,1,0:T(8,128)}) %all-gather.2.cloned.1.call-update) | async-done | bytes 8388624 | tf_op jit(solution)/shard_map/all_gather | solution.py:273
  157.6 2.8 broadcast_in_dim.9.old_ref
  160.4 12.0 %advance.4 = (bf16[16,1024,128]{2,1,0:T(8,128)(2,1)}, f32[4,8,128,128]{3,2,1,0:T(8,128)}) custom-call(s32[4]{0:T(128)} %copy-done.5, s32[4]{0:T(128)} %get-tuple-element.39.parents_ref, s32[16]{0:T(128)} %dynamic_slice.29.count_ref, bf16[16,512,128]{2,1,0:T(8,128)(2,1)} %bitcast.27, ...), custom_call_target="tpu_custom_call", output_to_operand_aliasing={{0}: (11, {})} | custom-call | flops 1610612736 | bytes 10485760 | tf_op jit(solution)/shard_map/advance/pallas_call | solution.py:221
  172.4 2.3 collective-permute-start
  174.7 12.0 %advance.5 = (bf16[16,1024,128]{2,1,0:T(8,128)(2,1)}, f32[4,8,128,128]{3,2,1,0:T(8,128)}) custom-call(s32[4]{0:T(128)} %copy-done.4, s32[4]{0:T(128)} %get-tuple-element.40.parents_ref, s32[16]{0:T(128)} %dynamic_slice.29.count_ref, bf16[16,512,128]{2,1,0:T(8,128)(2,1)} %bitcast.28, ...), custom_call_target="tpu_custom_call", output_to_operand_aliasing={{0}: (11, {})} | custom-call | flops 1610612736 | bytes 10485760 | tf_op jit(solution)/shard_map/advance/pallas_call | solution.py:221
  186.7 2.1 collective-permute-start.1
  188.8 0.6 and_select_fusion.2
  189.4 12.0 %advance.6 = (bf16[16,1024,128]{2,1,0:T(8,128)(2,1)}, f32[4,8,128,128]{3,2,1,0:T(8,128)}) custom-call(s32[4]{0:T(128)} %copy-done.3, s32[4]{0:T(128)} %get-tuple-element.41.parents_ref, s32[16]{0:T(128)} %dynamic_slice.29.count_ref, bf16[16,512,128]{2,1,0:T(8,128)(2,1)} %bitcast.29, ...), custom_call_target="tpu_custom_call", output_to_operand_aliasing={{0}: (11, {})} | custom-call | flops 1610612736 | bytes 10485760 | tf_op jit(solution)/shard_map/advance/pallas_call | solution.py:221
  201.4 0.1 collective-permute-start.2
  201.5 12.0 %advance.7 = (bf16[16,1024,128]{2,1,0:T(8,128)(2,1)}, f32[4,8,128,128]{3,2,1,0:T(8,128)}) custom-call(s32[4]{0:T(128)} %copy-done.2, s32[4]{0:T(128)} %get-tuple-element.42.parents_ref, s32[16]{0:T(128)} %dynamic_slice.29.count_ref, bf16[16,512,128]{2,1,0:T(8,128)(2,1)} %bitcast.30, ...), custom_call_target="tpu_custom_call", output_to_operand_aliasing={{0}: (11, {})} | custom-call | flops 1610612736 | bytes 10485760 | tf_op jit(solution)/shard_map/advance/pallas_call | solution.py:221
  213.5 51.1 %collective-permute-done = f32[4,8,128,128]{3,2,1,0:T(8,128)S(1)} collective-permute-done((f32[4,8,128,128]{3,2,1,0:T(8,128)}, f32[4,8,128,128]{3,2,1,0:T(8,128)S(1)}, u32[]{:S(2)}, u32[]{:S(2)}) %collective-permute-start) | collective-permute-done | bytes 2097184 | tf_op jit(solution)/shard_map/ppermute | solution.py:297
  264.6 1.0 broadcast_in_dim.10
  265.7 0.3 constant_dynamic-update-slice_fusion.3
  266.0 88.6 %collective-permute-done.1 = f32[4,8,128,128]{3,2,1,0:T(8,128)} collective-permute-done((f32[4,8,128,128]{3,2,1,0:T(8,128)}, f32[4,8,128,128]{3,2,1,0:T(8,128)}, u32[]{:S(2)}, u32[]{:S(2)}) %collective-permute-start.1) | collective-permute-done | bytes 2097184 | tf_op jit(solution)/shard_map/ppermute | solution.py:297
  354.5 1.8 constant_dynamic-update-slice_fusion.2
  356.4 1.8 constant_dynamic-update-slice_fusion.1
  358.2 0.3 constant_dynamic-update-slice_fusion
  358.6 3.4 copy-done
  (17 shorter events, 0.1 us)
Async XLA Ops:
  7.2 150.5 %all-gather.2.cloned.1.call-start = ((), (), s32[]{:S(2)}) async-start(), calls=%async_computation | async-start | bytes 10485760 | tf_op jit(solution)/shard_map/all_gather | solution.py:273
  9.5 118.4 %copy-start.4 = (s32[4]{0:T(128)}, s32[4]{0:T(128)S(1)}, u32[]{:S(2)}) copy-start(s32[4]{0:T(128)S(1)} %get-tuple-element.34.ids_ref) | copy-start | bytes 52
  9.5 118.4 %copy-start.5 = (s32[4]{0:T(128)}, s32[4]{0:T(128)S(1)}, u32[]{:S(2)}) copy-start(s32[4]{0:T(128)S(1)} %get-tuple-element.26.ids_ref) | copy-start | bytes 52
  9.5 179.3 %copy-start.2 = (s32[4]{0:T(128)}, s32[4]{0:T(128)S(1)}, u32[]{:S(2)}) copy-start(s32[4]{0:T(128)S(1)} %get-tuple-element.38.ids_ref) | copy-start | bytes 52
  9.5 179.3 %copy-start.3 = (s32[4]{0:T(128)}, s32[4]{0:T(128)S(1)}, u32[]{:S(2)}) copy-start(s32[4]{0:T(128)S(1)} %get-tuple-element.36.ids_ref) | copy-start | bytes 52
  172.4 92.2 %collective-permute-start = (f32[4,8,128,128]{3,2,1,0:T(8,128)}, f32[4,8,128,128]{3,2,1,0:T(8,128)S(1)}, u32[]{:S(2)}, u32[]{:S(2)}) collective-permute-start(f32[4,8,128,128]{3,2,1,0:T(8,128)} %get-tuple-element.21), channel_id=1, source_target_pairs={{0,8},{4,12},{8,0},{12,4},{1,9},{5,13},{9,1},{13,5},{2,10},{6,14},... | collective-permute-start | bytes 6291464 | tf_op jit(solution)/shard_map/ppermute | solution.py:297
  186.7 167.8 %collective-permute-start.1 = (f32[4,8,128,128]{3,2,1,0:T(8,128)}, f32[4,8,128,128]{3,2,1,0:T(8,128)}, u32[]{:S(2)}, u32[]{:S(2)}) collective-permute-start(f32[4,8,128,128]{3,2,1,0:T(8,128)} %get-tuple-element.22), channel_id=1, source_target_pairs={{0,4},{4,8},{8,12},{12,0},{1,5},{5,9},{9,13},{13,1},{2,6},{6,10},{... | collective-permute-start | bytes 6291464 | tf_op jit(solution)/shard_map/ppermute | solution.py:297
  201.4 155.0 %collective-permute-start.2 = (f32[4,8,128,128]{3,2,1,0:T(8,128)}, f32[4,8,128,128]{3,2,1,0:T(8,128)}, u32[]{:S(2)}, u32[]{:S(2)}) collective-permute-start(f32[4,8,128,128]{3,2,1,0:T(8,128)} %get-tuple-element.23), channel_id=1, source_target_pairs={{0,12},{4,0},{8,4},{12,8},{1,13},{5,1},{9,5},{13,9},{2,14},{6,2},{... | collective-permute-start | bytes 6291464 | tf_op jit(solution)/shard_map/ppermute | solution.py:297
  265.9 92.3 %copy-start.1 = (f32[4,8,128,128]{3,2,1,0:T(8,128)S(1)}, f32[4,8,128,128]{3,2,1,0:T(8,128)}, u32[]{:S(2)}) copy-start(f32[4,8,128,128]{3,2,1,0:T(8,128)} %get-tuple-element.24) | copy-start | bytes 6291460
  358.5 3.4 copy-start
Sparse Core Ops, SparseCore 0:
  9.6 148.0 all-gather.1
where the time goes:
time: 371 us; the launch traced here: 369 us
  waiting for transfers between devices  170 us (46%)
  Pallas kernels  158 us (43%)
  local copies, waits for them, and re-layouts  19.6 us (5%)
  between operations  14.2 us (4%)
  starting transfers between devices  4.52 us (1%)
    ppermute x3, waiting for transfers between devices, shards(): lax.ppermute(chunk, 'seq', [(d, (d + shift) % seq_count) for d in range(s...  140 us
    pallas_call x1, Pallas kernels, prepare(): pl.pallas_call(prepare_kernel, out_shape=(jax.ShapeDtypeStruct(square, F3...  110 us
    pallas_call x4, Pallas kernels, advance(): pl.pallas_call(advance_kernel, out_shape=(jax.ShapeDtypeStruct(mixed.shap...  47.9 us
    all_gather x1, waiting for transfers between devices, shards(): states = lax.all_gather(states, 'seq', axis=0, tiled=True)  29.7 us
  transfers between devices with their start and end apart: 4, of which 3 were waited for; matrix products, arithmetic and copies ran while one was open for 4% of the time, Pallas kernels for 40%

commit v1 on v0

--- a/solution.py
+++ b/solution.py
@@ -35,17 +35,60 @@
 def dot3(a, b):
     a_high, a_low = split(a)
     b_high, b_low = split(b)
-    return dot3_split(a_high, a_low, b_high, b_low)
-
-
-def dot3_split(a_high, a_low, b_high, b_low):
-    return dot(a_high, b_high) + dot(a_low, b_high) + dot(a_high, b_low)
-
-
-def prepare_kernel(count_ref, q_ref, k_ref, g_ref, b_ref, t_ref, m_ref, aux_ref,
+    right = jnp.concatenate([b_high, b_low], axis=1)
+    both = dot(jnp.concatenate([a_high, a_low], axis=1), jnp.concatenate([right, right], axis=0))
+    width = b.shape[1]
+    return both[:, :width] + both[:, width:]
+
+
+CODE_BITS = 15
+CODE_ROWS = 16
+
+
+def store_codes(code_ref, number, state):
+    rows = state.shape[0]
+    largest = jnp.maximum(jnp.max(jnp.abs(state), axis=0, keepdims=True), 1e-30)
+    power = jnp.ceil(jnp.log2(largest)) - CODE_BITS
+    limit = float(2**CODE_BITS - 1)
+    code = jnp.clip(jnp.round(state * jnp.exp2(-power)), -limit, limit)
+    code_ref[0, number * rows:(number + 1) * rows, :] = code.astype(jnp.int32).astype(jnp.int16)
+    return power
+
+
+def store_powers(code_ref, powers):
+    rows = code_ref.shape[1] - CODE_ROWS
+    spare = jnp.zeros((CODE_ROWS - len(powers), code_ref.shape[2]), F32)
+    table = jnp.concatenate(powers + [spare], axis=0)
+    code_ref[0, rows:, :] = table.astype(jnp.int32).astype(jnp.int16)
+
+
+def load_scales(code_ref):
+    rows = code_ref.shape[1] - CODE_ROWS
+    return jnp.exp2(code_ref[0, rows:, :].astype(jnp.int32).astype(F32))
+
+
+def load_state(code_ref, scales, number, rows):
+    code = code_ref[0, number * rows:(number + 1) * rows, :].astype(jnp.int32).astype(F32)
+    return code * scales[number:number + 1, :]
+
+
+def encode_kernel(state_ref, code_ref):
+    heads = state_ref.shape[1]
+    store_powers(code_ref, [store_codes(code_ref, h, state_ref[0, h]) for h in range(heads)])
+
+
+def decode_kernel(place_ref, code_ref, *refs):
+    del place_ref
+    state_ref = refs[-1]
+    heads, rows = state_ref.shape[1:3]
+    scales = load_scales(code_ref)
+    for h in range(heads):
+        state_ref[0, h] = load_state(code_ref, scales, h, rows)
+
+
+def prepare_kernel(ids_ref, count_ref, q_ref, k_ref, g_ref, b_ref, t_ref, m_ref, aux_ref,
                    q_rows, k_rows, a_rows):
-    number = pl.program_id(0)
-    live = count_ref[number]
+    live = count_ref[ids_ref[pl.program_id(0)]]
     length, value_heads = g_ref.shape[1:]
     key_heads = value_heads // 2
     q_rows[...] = q_ref[0].astype(F32)
@@ -96,21 +139,35 @@
         for h in range(value_heads):
             factor = jnp.take_along_axis(compact[h], index, axis=1)
             inverses[h] = inverses[h] - factor * inverses[h][j:j + 1, :]
+    block_masks = [lane // BASE == p for p in range(parts)]
+    levels = []
+    size = BASE
+    while size < length:
+        levels.append((size, range(size, length, 2 * size)))
+        size *= 2
     for h in range(value_heads):
-        a = a_rows[h]
-        result = jnp.concatenate(
-            [jnp.where(lane // BASE == p, inverses[h], 0.0) for p in range(parts)], axis=0
-        )
-        size = BASE
-        while size < length:
-            joined = (row // (2 * size) == col // (2 * size)) & (row // size != col // size)
-            cross = jnp.where(joined, a, 0.0)
-            result_high, result_low = split(result)
-            cross_high, cross_low = split(cross)
-            step = dot3_split(cross_high, cross_low, result_high, result_low)
-            step_high, step_low = split(step)
-            result = result - dot3_split(result_high, result_low, step_high, step_low)
-            size *= 2
+        blocks = [jnp.where(block_masks[p], inverses[h], 0.0) for p in range(parts)]
+        result = jnp.concatenate(blocks, axis=0)
+        for size, starts in levels:
+            lower = [
+                jnp.where(
+                    lax.broadcasted_iota(jnp.int32, (size, length), 1) // size == start // size - 1,
+                    a_rows[h, start:start + size, :],
+                    0.0,
+                )
+                for start in starts
+            ]
+            step = dot3(jnp.concatenate(lower, axis=0), result)
+            empty = jnp.zeros((size, length), F32)
+            spread = []
+            for n in range(len(starts)):
+                spread += [empty, step[n * size:(n + 1) * size]]
+            odd = jnp.concatenate([result[start:start + size] for start in starts], axis=0)
+            odd = odd - dot3(odd, jnp.concatenate(spread, axis=0))
+            joint = []
+            for n, start in enumerate(starts):
+                joint += [result[start - size:start], odd[n * size:(n + 1) * size]]
+            result = jnp.concatenate(joint, axis=0)
         t_ref[0, h] = result
     units = jnp.concatenate(unit_cols, axis=1)
     growth = jnp.exp(g_col)
@@ -118,15 +175,18 @@
     aux_ref[0] = jnp.concatenate([growth, b, b * growth * units, rest], axis=1)
 
 
-def advance_kernel(ids_ref, parents_ref, count_ref, q_ref, k_ref, v_ref, t_ref, m_ref, aux_ref,
-                   gain_ref, s_ref, old_ref, mixed_ref, state_ref,
-                   q_rows, k_rows, v_rows, o_rows):
-    del parents_ref, old_ref
+def advance_kernel(coded, ids_ref, parents_ref, count_ref, place_ref, q_ref, k_ref, v_ref, t_ref,
+                   m_ref, aux_ref, gain_ref, s_ref, *refs):
+    del parents_ref, place_ref
+    mixed_ref, state_ref, q_rows, k_rows, v_rows, o_rows = refs[-6:]
     number = ids_ref[pl.program_id(0)]
     live = count_ref[number]
     value_heads, length = t_ref.shape[1:3]
     key_heads = value_heads // 2
     width = s_ref.shape[-1]
+    key_dim = k_ref.shape[-1]
+    scales = load_scales(s_ref)
+    powers = []
     q_rows[...] = q_ref[0].astype(F32)
     k_rows[...] = k_ref[0].astype(F32)
     v_rows[...] = v_ref[0].astype(F32)
@@ -136,7 +196,8 @@
     for m in range(key_heads):
         q = q_rows[pl.ds(m, length, stride=key_heads), :].astype(BF16)
         k = k_rows[pl.ds(m, length, stride=key_heads), :].astype(BF16)
-        s = jnp.concatenate([s_ref[0, 2 * m], s_ref[0, 2 * m + 1]], axis=1)
+        states = [load_state(s_ref, scales, 2 * m + r, key_dim) for r in range(2)]
+        s = jnp.concatenate(states, axis=1)
         s_high, s_low = split(s)
         kq = jnp.concatenate([k, q], axis=0)
         applied = dot(jnp.concatenate([kq, kq], axis=1), jnp.concatenate([s_high, s_low], axis=0))
@@ -161,15 +222,23 @@
         for r in range(2):
             h = 2 * m + r
             last = aux[length - 1:length, h:h + 1]
-            state_ref[0, h] = last * s_ref[0, h] + added[:, r * width:(r + 1) * width]
+            state = last * states[r] + added[:, r * width:(r + 1) * width]
+            if coded:
+                powers.append(store_codes(state_ref, h, state))
+            else:
+                state_ref[0, h] = state
+    if coded:
+        store_powers(state_ref, powers)
     mixed_ref[0] = o_rows[...].astype(BF16)
 
 
-def prepare(counts, queries, keys, decay, rate):
-    expansions, length, value_heads = decay.shape
+def prepare(ids, counts, queries, keys, decay, rate):
+    expansions = ids.shape[0]
+    length, value_heads = decay.shape[1:]
     rows, key_dim = queries.shape[1:]
     square = (expansions, value_heads, length, length)
-    block = lambda shape: pl.BlockSpec((1,) + shape, lambda i, c: (i,) + (0,) * len(shape))
+    own = lambda shape: pl.BlockSpec((1,) + shape, lambda i, ids, c: (ids[i],) + (0,) * len(shape))
+    block = lambda shape: pl.BlockSpec((1,) + shape, lambda i, ids, c: (i,) + (0,) * len(shape))
     work = expansions * value_heads
     return pl.pallas_call(
         prepare_kernel,
@@ -179,13 +248,13 @@
             jax.ShapeDtypeStruct((expansions, length, 4 * value_heads), F32),
         ),
         grid_spec=pltpu.PrefetchScalarGridSpec(
-            num_scalar_prefetch=1,
+            num_scalar_prefetch=2,
             grid=(expansions,),
             in_specs=[
-                block((rows, key_dim)),
-                block((rows, key_dim)),
-                block((length, value_heads)),
-                block((length, value_heads)),
+                own((rows, key_dim)),
+                own((rows, key_dim)),
+                own((length, value_heads)),
+                own((length, value_heads)),
             ],
             out_specs=(
                 block(square[1:]),
@@ -205,43 +274,93 @@
             transcendentals=work * length * length,
         ),
         name="prepare",
-    )(counts, queries, keys, decay, rate)
-
-
-def advance(ids, parents, counts, queries, keys, values, inverse, mixing, aux, gain, states, mixed):
+    )(ids, counts, queries, keys, decay, rate)
+
+
+def encode(states):
+    count, heads, key_dim, width = states.shape
+    rows = heads * key_dim + CODE_ROWS
+    return pl.pallas_call(
+        encode_kernel,
+        out_shape=jax.ShapeDtypeStruct((count, rows, width), jnp.int16),
+        grid=(count,),
+        in_specs=[pl.BlockSpec((1, heads, key_dim, width), lambda i: (i, 0, 0, 0))],
+        out_specs=pl.BlockSpec((1, rows, width), lambda i: (i, 0, 0)),
+        compiler_params=pltpu.CompilerParams(vmem_limit_bytes=VMEM_BYTES),
+        name="encode",
+    )(states)
+
+
+def decode(place, codes, final):
+    count, rows, width = codes.shape
+    heads, key_dim = final.shape[1:3]
+    return pl.pallas_call(
+        decode_kernel,
+        out_shape=jax.ShapeDtypeStruct(final.shape, final.dtype),
+        grid_spec=pltpu.PrefetchScalarGridSpec(
+            num_scalar_prefetch=1,
+            grid=(count,),
+            in_specs=[
+                pl.BlockSpec((1, rows, width), lambda i, place: (i, 0, 0)),
+                pl.BlockSpec(memory_space=pl.ANY),
+            ],
+            out_specs=pl.BlockSpec(
+                (1, heads, key_dim, width), lambda i, place: (place[0] + i, 0, 0, 0)
+            ),
+        ),
+        input_output_aliases={2: 0},
+        compiler_params=pltpu.CompilerParams(vmem_limit_bytes=VMEM_BYTES),
+        name="decode",
+    )(place, codes, final)
+
+
+def advance(ids, parents, counts, place, first, queries, keys, values, inverse, mixing, aux, gain,
+            states, mixed, coded):
     steps = ids.shape[0]
+    expansions = queries.shape[0]
     value_heads, length = inverse.shape[1:3]
     rows, key_dim = queries.shape[1:]
-    width = states.shape[-1]
+    width = values.shape[-1]
+    state_rows = states.shape[1]
     own = lambda shape: pl.BlockSpec(
-        (1,) + shape, lambda i, ids, par, c: (ids[i],) + (0,) * len(shape)
+        (1,) + shape, lambda i, ids, par, c, p: (ids[i],) + (0,) * len(shape)
     )
-    state_block = (1, value_heads, key_dim, width)
+    step = lambda shape: pl.BlockSpec(
+        (1,) + shape, lambda i, ids, par, c, p: (first + i,) + (0,) * len(shape)
+    )
+    if coded:
+        state_shape = jax.ShapeDtypeStruct((steps, state_rows, width), jnp.int16)
+        state_spec = pl.BlockSpec((1, state_rows, width), lambda i, ids, par, c, p: (i, 0, 0))
+    else:
+        state_shape = jax.ShapeDtypeStruct((expansions, value_heads, key_dim, width), F32)
+        state_spec = pl.BlockSpec(
+            (1, value_heads, key_dim, width), lambda i, ids, par, c, p: (p[0] + i, 0, 0, 0)
+        )
+    in_specs = [
+        own((rows, key_dim)),
+        own((rows, key_dim)),
+        own((length * value_heads, width)),
+        step((value_heads, length, length)),
+        step((value_heads, length, length)),
+        step((length, 4 * value_heads)),
+        pl.BlockSpec((1, width), lambda i, ids, par, c, p: (0, 0)),
+        pl.BlockSpec((1, state_rows, width), lambda i, ids, par, c, p: (par[i], 0, 0)),
+    ]
+    operands = [ids, parents, counts, place, queries, keys, values, inverse, mixing, aux, gain, states]
+    aliases = {}
+    if mixed is not None:
+        aliases = {len(operands): 0}
+        operands.append(mixed)
+        in_specs.append(pl.BlockSpec(memory_space=pl.ANY))
     work = steps * value_heads
     return pl.pallas_call(
-        advance_kernel,
-        out_shape=(
-            jax.ShapeDtypeStruct(mixed.shape, mixed.dtype),
-            jax.ShapeDtypeStruct((steps,) + state_block[1:], F32),
-        ),
+        functools.partial(advance_kernel, coded),
+        out_shape=(jax.ShapeDtypeStruct(values.shape, BF16), state_shape),
         grid_spec=pltpu.PrefetchScalarGridSpec(
-            num_scalar_prefetch=3,
+            num_scalar_prefetch=4,
             grid=(steps,),
-            in_specs=[
-                own((rows, key_dim)),
-                own((rows, key_dim)),
-                own((length * value_heads, width)),
-                own((value_heads, length, length)),
-                own((value_heads, length, length)),
-                own((length, 4 * value_heads)),
-                pl.BlockSpec((1, width), lambda i, ids, par, c: (0, 0)),
-                pl.BlockSpec(state_block, lambda i, ids, par, c: (par[i], 0, 0, 0)),
-                pl.BlockSpec(memory_space=pl.ANY),
-            ],
-            out_specs=(
-                own((length * value_heads, width)),
-                pl.BlockSpec(state_block, lambda i, ids, par, c: (i, 0, 0, 0)),
-            ),
+            in_specs=in_specs,
+            out_specs=(own((length * value_heads, width)), state_spec),
             scratch_shapes=[
                 pltpu.VMEM((rows, key_dim), F32),
                 pltpu.VMEM((rows, key_dim), F32),
@@ -249,7 +368,7 @@
                 pltpu.VMEM((length * value_heads, width), F32),
             ],
         ),
-        input_output_aliases={11: 0},
+        input_output_aliases=aliases,
         compiler_params=pltpu.CompilerParams(vmem_limit_bytes=VMEM_BYTES),
         cost_estimate=pl.CostEstimate(
             flops=work * 12 * 2 * length**3,
@@ -257,7 +376,7 @@
             transcendentals=work * length,
         ),
         name="advance",
-    )(ids, parents, counts, queries, keys, values, inverse, mixing, aux, gain, states, mixed)
+    )(*operands)
 
 
 def shards(queries, keys, values, log_decay, write_rate, norm_gain, parent_cache, order,
@@ -269,8 +388,8 @@
     width = values.shape[-1]
     per_peer = expansions // seq_count
     cache_rows = parent_cache.shape[0]
-    states = parent_cache.reshape(cache_rows, value_heads, key_dim, width)
-    states = lax.all_gather(states, "seq", axis=0, tiled=True)
+    codes = encode(parent_cache.reshape(cache_rows, value_heads, key_dim, width))
+    states = lax.all_gather(codes, "seq", axis=0, tiled=True)
     start = me * expansions
     own = lambda table: lax.dynamic_slice_in_dim(table, start, expansions)
     counts = own(token_count)
@@ -278,27 +397,36 @@
     sends = lax.dynamic_slice_in_dim(
         order.reshape(seq_count, expansions), me * per_peer, per_peer, 1
     ) - start
+    shifts = sorted(range(seq_count), key=lambda s: -min(s, seq_count - s))
+    targets = lax.rem(me + jnp.array(shifts, jnp.int32), seq_count)
+    ids = jnp.take(sends, targets, axis=0).reshape(-1)
+    parents = jnp.take(parents, ids)
+    remote = expansions - per_peer
     q = queries.reshape(expansions, length * key_heads, key_dim)
     k = keys.reshape(expansions, length * key_heads, key_dim)
     v = values.reshape(expansions, length * value_heads, width)
     decay = log_decay.reshape(expansions, length, value_heads)
     rate = write_rate.reshape(expansions, length, value_heads)
-    inverse, mixing, aux = prepare(counts, q, k, decay, rate)
-    mixed = jnp.zeros((expansions, length * value_heads, width), BF16)
     gain = norm_gain.reshape(1, width)
-    final = jnp.zeros((expansions, value_heads, key_dim, width), F32)
-    shifts = sorted(range(seq_count), key=lambda s: -min(s, seq_count - s))
-    for shift in shifts:
-        target = lax.rem(me + shift, seq_count)
-        ids = lax.dynamic_index_in_dim(sends, target, 0, keepdims=False)
-        mixed, chunk = advance(ids, jnp.take(parents, ids), counts, q, k, v, inverse, mixing, aux,
-                               gain, states, mixed)
+    pieces = prepare(ids[:remote], counts, q, k, decay, rate)
+    mixed = None
+    arriving = []
+    for at, shift in enumerate(shifts):
+        first = at * per_peer
+        if not shift:
+            late, _ = lax.optimization_barrier((ids[remote:], codes))
+            pieces = prepare(late, counts, q, k, decay, rate)
+            first = 0
+        here = slice(at * per_peer, (at + 1) * per_peer)
+        place = (lax.rem(me + seq_count - shift, seq_count) * per_peer).reshape(1)
+        mixed, codes = advance(ids[here], parents[here], counts, place, first, q, k, v, *pieces,
+                               gain, states, mixed, bool(shift))
         if shift:
-            chunk = lax.ppermute(
-                chunk, "seq", [(d, (d + shift) % seq_count) for d in range(seq_count)]
-            )
-        source = lax.rem(me + seq_count - shift, seq_count)
-        final = lax.dynamic_update_slice_in_dim(final, chunk, source * per_peer, 0)
+            pairs = [(d, (d + shift) % seq_count) for d in range(seq_count)]
+            arriving.append((place, lax.ppermute(codes, "seq", pairs)))
+    final = codes
+    for place, codes in arriving:
+        final = decode(place, codes, final)
     return (
         mixed.reshape(values.shape),
         final.reshape((expansions,) + parent_cache.shape[1:]),

time: 371 us -> 303 us (0.82)
  waiting for transfers between devices: 170 us -> 38.9 us
  blocking collectives: 0 us -> 79.8 us
  between operations: 14.2 us -> 0.66 us
  local copies, waits for them, and re-layouts: 19.6 us -> 11.7 us
  Pallas kernels: 158 us -> 163 us
    ppermute x3, waiting for transfers between devices: 140 us -> 38.9 us  [shards(): arriving.append((place, lax.ppermute(codes, 'seq', pairs)))]
    all_gather x0 -> x1, blocking collectives: none -> 79.8 us  [shards(): states = lax.all_gather(codes, 'seq', axis=0, tiled=True)]
    all_gather x1 -> x0, waiting for transfers between devices: 29.7 us -> none  [shards(): states = lax.all_gather(states, 'seq', axis=0, tiled=True)]
    pallas_call x4 -> x8, Pallas kernels: 47.9 us -> 61.8 us  [the longest x4 47.2 us: advance(): pl.pallas_call(functools.partial(advance_kernel, coded), out_shape=(jax.S...]
    pallas_call x1 -> x2, Pallas kernels: 110 us -> 101 us  [prepare(): pl.pallas_call(prepare_kernel, out_shape=(jax.ShapeDtypeStruct(square, F3...]
    dynamic_update_slice x4 -> x0, local copies, waits for them, and re-layouts: 4.24 us -> none  [shards(): final = lax.dynamic_update_slice_in_dim(final, chunk, source * per_peer, 0)]
    broadcast_in_dim x2 -> x0, local copies, waits for them, and re-layouts: 3.86 us -> none  [the longest x1 2.82 us: shards(): mixed = jnp.zeros((expansions, length * value_heads, width), BF16)]
  transfers between devices with their start and end apart: 4 -> 3, of which waited for: 3 -> 1; matrix products, arithmetic and copies ran while one was open for 4% -> 0% of each run, Pallas kernels for 40% -> 19%
where the time goes in v1:
time: 303 us; the launch traced here: 299 us
  Pallas kernels  163 us (54%)
  blocking collectives  79.8 us (26%)
  waiting for transfers between devices  38.9 us (13%)
  local copies, waits for them, and re-layouts  11.7 us (4%)
  starting transfers between devices  3.52 us (1%)
    pallas_call x2, Pallas kernels, prepare(): pl.pallas_call(prepare_kernel, out_shape=(jax.ShapeDtypeStruct(square, F3...  101 us
    all_gather x1, blocking collectives, shards(): states = lax.all_gather(codes, 'seq', axis=0, tiled=True)  79.8 us
    pallas_call x4, Pallas kernels, advance(): pl.pallas_call(functools.partial(advance_kernel, coded), out_shape=(jax.S...  47.2 us
    ppermute x3, waiting for transfers between devices, shards(): arriving.append((place, lax.ppermute(codes, 'seq', pairs)))  38.9 us
    pallas_call x3, Pallas kernels, decode(): pl.pallas_call(decode_kernel, out_shape=jax.ShapeDtypeStruct(final.shape,...  10.8 us
  transfers between devices with their start and end apart: 3, of which 1 were waited for; matrix products, arithmetic and copies ran while one was open for 0% of the time, Pallas kernels for 19%

profile of v1, /device:TPU:11, one launch (start us, length us, event | category | flops | bytes accessed | tf_op | source)
XLA Modules:
  0.0 299.5 jit_solution(8915972793049123141)
XLA Ops:
  0.6 0.7 compare_and_fusion
  1.3 0.7 reshape.97
  2.1 0.6 gather_fusion
  2.7 0.1 broadcast_select_fusion
  2.8 0.1 select_n.59
  2.8 0.1 select_n.56
  2.9 0.6 slice_bitcast_fusion
  3.5 0.6 slice.50.ids_ref
  4.1 1.3 dynamic_slice.15.count_ref
  5.4 0.7 dynamic-slice_add_fusion
  6.1 0.7 gather_fusion.1
  6.8 0.6 fusion.2
  7.4 1.8 copy.30.g_ref
  9.2 1.8 copy.31.b_ref
  11.0 3.8 %encode.1 = s16[4,1040,128]{2,1,0:T(8,128)(2,1)} custom-call(f32[4,8,128,128]{3,2,1,0:T(8,128)} %bitcast.42), custom_call_target="tpu_custom_call" | custom-call | tf_op jit(solution)/shard_map/encode/pallas_call | solution.py:283
  14.7 79.8 %all-gather.1.s_ref = s16[16,1040,128]{2,1,0:T(8,128)(2,1)} all-gather(s16[4,1040,128]{2,1,0:T(8,128)(2,1)} %encode.1), channel_id=1, replica_groups=mesh['groups'=2,'seq'=4,'head'=2,'sub'=2] {'seq'}, dimensions={0}, use_global_device_ids=true | all-gather | bytes 5324800 | tf_op jit(solution)/shard_map/all_gather | solution.py:392
  94.5 74.9 %prepare.2 = (f32[12,8,128,128]{3,2,1,0:T(8,128)}, f32[12,8,128,128]{3,2,1,0:T(8,128)}, f32[12,128,32]{2,1,0:T(8,128)}) custom-call(s32[12]{0:T(128)} %slice.50.ids_ref, s32[16]{0:T(128)} %dynamic_slice.15.count_ref, bf16[16,512,128]{2,1,0:T(8,128)(2,1)} %bitcast.30, bf16[16,512,128]{2,1,0:T(8,128)(2,1)} %bitcast.36, bf16[16,128,8]{2,1,0:T(8,128)(2,1)} %copy.30.g_ref, ...), custom_call_target="tpu_custom_call" | custom-call | flops 12079595520 | bytes 12582912 | tf_op jit(solution)/shard_map/prepare/pallas_call | solution.py:243
  169.4 11.8 %advance.4 = (bf16[16,1024,128]{2,1,0:T(8,128)(2,1)}, s16[4,1040,128]{2,1,0:T(8,128)(2,1)}) custom-call(s32[4]{0:T(128)} %get-tuple-element.34.ids_ref, s32[4]{0:T(128)} %get-tuple-element.38.parents_ref, s32[16]{0:T(128)} %dynamic_slice.15.count_ref, s32[1]{0:T(128)} %bitcast.15.place_ref, bf16[16,512,128]{2,1,0:T(8,128)(2,1)} %bitcast.31, ...), custom_call_target="tpu_custom_call" | custom-call | flops 1610612736 | bytes 10485760 | tf_op jit(solution)/shard_map/advance/pallas_call | solution.py:356
  181.2 11.8 %advance.5 = (bf16[16,1024,128]{2,1,0:T(8,128)(2,1)}, s16[4,1040,128]{2,1,0:T(8,128)(2,1)}) custom-call(s32[4]{0:T(128)} %get-tuple-element.35.ids_ref, s32[4]{0:T(128)} %get-tuple-element.39.parents_ref, s32[16]{0:T(128)} %dynamic_slice.15.count_ref, s32[1]{0:T(128)} %bitcast.13.place_ref, ...), custom_call_target="tpu_custom_call", output_to_operand_aliasing={{0}: (12, {})} | custom-call | flops 1610612736 | bytes 10485760 | tf_op jit(solution)/shard_map/advance/pallas_call | solution.py:356
  193.1 2.2 collective-permute-start.1
  195.3 0.1 collective-permute-start.2
  195.4 11.8 %advance.6 = (bf16[16,1024,128]{2,1,0:T(8,128)(2,1)}, s16[4,1040,128]{2,1,0:T(8,128)(2,1)}) custom-call(s32[4]{0:T(128)} %get-tuple-element.36.ids_ref, s32[4]{0:T(128)} %get-tuple-element.40.parents_ref, s32[16]{0:T(128)} %dynamic_slice.15.count_ref, s32[1]{0:T(128)} %bitcast.7.place_ref, ...), custom_call_target="tpu_custom_call", output_to_operand_aliasing={{0}: (12, {})} | custom-call | flops 1610612736 | bytes 10485760 | tf_op jit(solution)/shard_map/advance/pallas_call | solution.py:356
  207.3 1.2 collective-permute-start
  208.5 26.6 %prepare.3 = (f32[4,8,128,128]{3,2,1,0:T(8,128)}, f32[4,8,128,128]{3,2,1,0:T(8,128)}, f32[4,128,32]{2,1,0:T(8,128)}) custom-call(s32[4]{0:T(128)} %get-tuple-element.23.ids_ref, s32[16]{0:T(128)} %dynamic_slice.15.count_ref, bf16[16,512,128]{2,1,0:T(8,128)(2,1)} %bitcast.34, bf16[16,512,128]{2,1,0:T(8,128)(2,1)} %bitcast.40, ...), custom_call_target="tpu_custom_call" | custom-call | flops 4026531840 | bytes 4194304 | tf_op jit(solution)/shard_map/prepare/pallas_call | solution.py:243
  235.0 11.7 %advance.7 = (bf16[16,1024,128]{2,1,0:T(8,128)(2,1)}, f32[16,8,128,128]{3,2,1,0:T(8,128)}) custom-call(s32[4]{0:T(128)} %get-tuple-element.23.ids_ref, s32[4]{0:T(128)} %get-tuple-element.41.parents_ref, s32[16]{0:T(128)} %dynamic_slice.15.count_ref, s32[1]{0:T(128)} %bitcast.2.place_ref, ...), custom_call_target="tpu_custom_call", output_to_operand_aliasing={{0}: (12, {})} | custom-call | flops 1610612736 | bytes 10485760 | tf_op jit(solution)/shard_map/advance/pallas_call | solution.py:356
  246.7 38.9 %collective-permute-done.2.code_ref = s16[4,1040,128]{2,1,0:T(8,128)(2,1)S(1)} collective-permute-done((s16[4,1040,128]{2,1,0:T(8,128)(2,1)}, s16[4,1040,128]{2,1,0:T(8,128)(2,1)S(1)}, u32[]{:S(2)}, u32[]{:S(2)}) %collective-permute-start.2) | collective-permute-done | bytes 1064992 | tf_op jit(solution)/shard_map/ppermute | solution.py:426
  285.6 1.0 copy-done.1
  286.6 3.6 %decode.3.refs_0_ = f32[16,8,128,128]{3,2,1,0:T(8,128)} custom-call(s32[1]{0:T(128)} %bitcast.15.place_ref, s16[4,1040,128]{2,1,0:T(8,128)(2,1)} %copy-done.1, f32[16,8,128,128]{3,2,1,0:T(8,128)} %get-tuple-element.31.refs_0_), custom_call_target="tpu_custom_call", output_to_operand_aliasing={{}: (2, {})} | custom-call | tf_op jit(solution)/shard_map/decode/pallas_call | solution.py:297
  290.3 1.0 copy-done
  291.2 3.6 %decode.4.refs_0_ = f32[16,8,128,128]{3,2,1,0:T(8,128)} custom-call(s32[1]{0:T(128)} %bitcast.13.place_ref, s16[4,1040,128]{2,1,0:T(8,128)(2,1)} %copy-done, f32[16,8,128,128]{3,2,1,0:T(8,128)} %decode.3.refs_0_), custom_call_target="tpu_custom_call", output_to_operand_aliasing={{}: (2, {})} | custom-call | tf_op jit(solution)/shard_map/decode/pallas_call | solution.py:297
  294.9 1.0 copy-done.2
  295.8 3.6 %decode.5 = f32[16,8,128,128]{3,2,1,0:T(8,128)} custom-call(s32[1]{0:T(128)} %bitcast.7.place_ref, s16[4,1040,128]{2,1,0:T(8,128)(2,1)} %copy-done.2, f32[16,8,128,128]{3,2,1,0:T(8,128)} %decode.4.refs_0_), custom_call_target="tpu_custom_call", output_to_operand_aliasing={{}: (2, {})} | custom-call | tf_op jit(solution)/shard_map/decode/pallas_call | solution.py:297
  (10 shorter events, 0.1 us)
Async XLA Ops:
  193.1 97.2 %collective-permute-start.1 = (s16[4,1040,128]{2,1,0:T(8,128)(2,1)}, s16[4,1040,128]{2,1,0:T(8,128)(2,1)S(1)}, u32[]{:S(2)}, u32[]{:S(2)}) collective-permute-start(s16[4,1040,128]{2,1,0:T(8,128)(2,1)} %get-tuple-element.29), channel_id=1, source_target_pairs={{0,4},{4,8},{8,12},{12,0},{1,5},{5,9},{9,13},{13,1},{2,6},{6,10},{... | collective-permute-start | bytes 3194888 | tf_op jit(solution)/shard_map/ppermute | solution.py:426
  195.3 90.4 %collective-permute-start.2 = (s16[4,1040,128]{2,1,0:T(8,128)(2,1)}, s16[4,1040,128]{2,1,0:T(8,128)(2,1)S(1)}, u32[]{:S(2)}, u32[]{:S(2)}) collective-permute-start(s16[4,1040,128]{2,1,0:T(8,128)(2,1)} %get-tuple-element.30), channel_id=1, source_target_pairs={{0,8},{4,12},{8,0},{12,4},{1,9},{5,13},{9,1},{13,5},{2,10},{6,14},... | collective-permute-start | bytes 3194888 | tf_op jit(solution)/shard_map/ppermute | solution.py:426
  207.3 87.6 %collective-permute-start = (s16[4,1040,128]{2,1,0:T(8,128)(2,1)}, s16[4,1040,128]{2,1,0:T(8,128)(2,1)S(1)}, u32[]{:S(2)}, u32[]{:S(2)}) collective-permute-start(s16[4,1040,128]{2,1,0:T(8,128)(2,1)} %get-tuple-element.22), channel_id=1, source_target_pairs={{0,12},{4,0},{8,4},{12,8},{1,13},{5,1},{9,5},{13,9},{2,14},{6,2},{... | collective-permute-start | bytes 3194888 | tf_op jit(solution)/shard_map/ppermute | solution.py:426
  285.6 1.0 copy-start.1
  290.3 1.0 copy-start
  294.9 1.0 copy-start.2

commit v2 on v1

--- a/solution.py
+++ b/solution.py
@@ -42,39 +42,46 @@
 
 
 CODE_BITS = 15
-CODE_ROWS = 16
-
-
-def store_codes(code_ref, number, state):
-    rows = state.shape[0]
+CODE_ROWS = 8
+
+
+def code_state(state):
     largest = jnp.maximum(jnp.max(jnp.abs(state), axis=0, keepdims=True), 1e-30)
     power = jnp.ceil(jnp.log2(largest)) - CODE_BITS
     limit = float(2**CODE_BITS - 1)
     code = jnp.clip(jnp.round(state * jnp.exp2(-power)), -limit, limit)
-    code_ref[0, number * rows:(number + 1) * rows, :] = code.astype(jnp.int32).astype(jnp.int16)
-    return power
+    return code.astype(jnp.int32), power.astype(jnp.int32)
+
+
+def store_pair(code_ref, pair, states):
+    (low, low_power), (high, high_power) = [code_state(state) for state in states]
+    rows = low.shape[0]
+    code_ref[0, pair * rows:(pair + 1) * rows, :] = (high << 16) | (low & 0xFFFF)
+    return [low_power, high_power]
 
 
 def store_powers(code_ref, powers):
     rows = code_ref.shape[1] - CODE_ROWS
-    spare = jnp.zeros((CODE_ROWS - len(powers), code_ref.shape[2]), F32)
-    table = jnp.concatenate(powers + [spare], axis=0)
-    code_ref[0, rows:, :] = table.astype(jnp.int32).astype(jnp.int16)
+    spare = [jnp.zeros_like(powers[0])] * (CODE_ROWS - len(powers))
+    code_ref[0, rows:, :] = jnp.concatenate(powers + spare, axis=0)
 
 
 def load_scales(code_ref):
     rows = code_ref.shape[1] - CODE_ROWS
-    return jnp.exp2(code_ref[0, rows:, :].astype(jnp.int32).astype(F32))
-
-
-def load_state(code_ref, scales, number, rows):
-    code = code_ref[0, number * rows:(number + 1) * rows, :].astype(jnp.int32).astype(F32)
-    return code * scales[number:number + 1, :]
+    return jnp.exp2(code_ref[0, rows:, :].astype(F32))
+
+
+def load_pair(code_ref, scales, pair, rows):
+    word = code_ref[0, pair * rows:(pair + 1) * rows, :]
+    codes = [(word << 16) >> 16, word >> 16]
+    return [c.astype(F32) * scales[2 * pair + r:2 * pair + r + 1, :] for r, c in enumerate(codes)]
 
 
 def encode_kernel(state_ref, code_ref):
-    heads = state_ref.shape[1]
-    store_powers(code_ref, [store_codes(code_ref, h, state_ref[0, h]) for h in range(heads)])
+    powers = []
+    for m in range(state_ref.shape[1] // 2):
+        powers += store_pair(code_ref, m, [state_ref[0, 2 * m], state_ref[0, 2 * m + 1]])
+    store_powers(code_ref, powers)
 
 
 def decode_kernel(place_ref, code_ref, *refs):
@@ -82,8 +89,8 @@
     state_ref = refs[-1]
     heads, rows = state_ref.shape[1:3]
     scales = load_scales(code_ref)
-    for h in range(heads):
-        state_ref[0, h] = load_state(code_ref, scales, h, rows)
+    for m in range(heads // 2):
+        state_ref[0, 2 * m], state_ref[0, 2 * m + 1] = load_pair(code_ref, scales, m, rows)
 
 
 def prepare_kernel(ids_ref, count_ref, q_ref, k_ref, g_ref, b_ref, t_ref, m_ref, aux_ref,
@@ -196,7 +203,7 @@
     for m in range(key_heads):
         q = q_rows[pl.ds(m, length, stride=key_heads), :].astype(BF16)
         k = k_rows[pl.ds(m, length, stride=key_heads), :].astype(BF16)
-        states = [load_state(s_ref, scales, 2 * m + r, key_dim) for r in range(2)]
+        states = load_pair(s_ref, scales, m, key_dim)
         s = jnp.concatenate(states, axis=1)
         s_high, s_low = split(s)
         kq = jnp.concatenate([k, q], axis=0)
@@ -219,14 +226,15 @@
         update = jnp.concatenate(updates, axis=1)
         u_high, u_low = split(update)
         added = dot_tn(jnp.concatenate([k, k], axis=0), jnp.concatenate([u_high, u_low], axis=0))
+        later = []
         for r in range(2):
             h = 2 * m + r
             last = aux[length - 1:length, h:h + 1]
-            state = last * states[r] + added[:, r * width:(r + 1) * width]
-            if coded:
-                powers.append(store_codes(state_ref, h, state))
-            else:
-                state_ref[0, h] = state
+            later.append(last * states[r] + added[:, r * width:(r + 1) * width])
+        if coded:
+            powers += store_pair(state_ref, m, later)
+        else:
+            state_ref[0, 2 * m], state_ref[0, 2 * m + 1] = later
     if coded:
         store_powers(state_ref, powers)
     mixed_ref[0] = o_rows[...].astype(BF16)
@@ -279,10 +287,10 @@
 
 def encode(states):
     count, heads, key_dim, width = states.shape
-    rows = heads * key_dim + CODE_ROWS
+    rows = heads // 2 * key_dim + CODE_ROWS
     return pl.pallas_call(
         encode_kernel,
-        out_shape=jax.ShapeDtypeStruct((count, rows, width), jnp.int16),
+        out_shape=jax.ShapeDtypeStruct((count, rows, width), jnp.int32),
         grid=(count,),
         in_specs=[pl.BlockSpec((1, heads, key_dim, width), lambda i: (i, 0, 0, 0))],
         out_specs=pl.BlockSpec((1, rows, width), lambda i: (i, 0, 0)),
@@ -329,7 +337,7 @@
         (1,) + shape, lambda i, ids, par, c, p: (first + i,) + (0,) * len(shape)
     )
     if coded:
-        state_shape = jax.ShapeDtypeStruct((steps, state_rows, width), jnp.int16)
+        state_shape = jax.ShapeDtypeStruct((steps, state_rows, width), jnp.int32)
         state_spec = pl.BlockSpec((1, state_rows, width), lambda i, ids, par, c, p: (i, 0, 0))
     else:
         state_shape = jax.ShapeDtypeStruct((expansions, value_heads, key_dim, width), F32)

time: 303 us -> 231 us (0.76)
  blocking collectives: 79.8 us -> 0 us
  between operations: 0.66 us -> 14.2 us
    all_gather x1 -> x0, blocking collectives: 79.8 us -> none  [shards(): states = lax.all_gather(codes, 'seq', axis=0, tiled=True)]
  transfers between devices with their start and end apart: 3 -> 4, of which waited for: 1 -> 1; matrix products, arithmetic and copies ran while one was open for 0% -> 3% of each run, Pallas kernels for 19% -> 58%
where the time goes in v2:
time: 231 us; the launch traced here: 229 us
  Pallas kernels  163 us (71%)
  waiting for transfers between devices  38.1 us (16%)
  between operations  14.2 us (6%)
  local copies, waits for them, and re-layouts  9.1 us (4%)
  starting transfers between devices  4.43 us (2%)
    pallas_call x2, Pallas kernels, prepare(): pl.pallas_call(prepare_kernel, out_shape=(jax.ShapeDtypeStruct(square, F3...  101 us
    pallas_call x4, Pallas kernels, advance(): pl.pallas_call(functools.partial(advance_kernel, coded), out_shape=(jax.S...  47.1 us
    ppermute x3, waiting for transfers between devices, shards(): arriving.append((place, lax.ppermute(codes, 'seq', pairs)))  38 us
    pallas_call x3, Pallas kernels, decode(): pl.pallas_call(decode_kernel, out_shape=jax.ShapeDtypeStruct(final.shape,...  10.9 us
  transfers between devices with their start and end apart: 4, of which 1 were waited for; matrix products, arithmetic and copies ran while one was open for 3% of the time, Pallas kernels for 58%

profile of v2, /device:TPU:11, one launch (start us, length us, event | category | flops | bytes accessed | tf_op | source)
XLA Modules:
  0.0 229.3 jit_solution(8558970715198290651)
XLA Ops:
  7.2 0.0 all-gather.2.cloned.1.call-start
  7.3 3.8 %encode.1 = s32[4,520,128]{2,1,0:T(8,128)} custom-call(f32[4,8,128,128]{3,2,1,0:T(8,128)} %bitcast.42), custom_call_target="tpu_custom_call" | custom-call | tf_op jit(solution)/shard_map/encode/pallas_call | solution.py:291
  11.1 0.1 reshape.97
  11.2 0.1 dynamic-slice_subtract_fusion
  11.3 0.6 gather_fusion
  11.8 0.1 broadcast_select_fusion
  11.9 0.1 select_n.59
  12.0 0.1 select_n.56
  12.1 0.6 slice.50.ids_ref
  12.7 1.0 copy.30.g_ref
  13.7 1.0 copy.31.b_ref
  14.8 0.6 dynamic_slice.15.count_ref
  15.4 0.1 dynamic-slice_add_fusion
  15.5 0.7 gather_fusion.1
  16.2 0.7 fusion.2
  16.9 0.6 slice_bitcast_fusion
  17.4 74.9 %prepare.2 = (f32[12,8,128,128]{3,2,1,0:T(8,128)}, f32[12,8,128,128]{3,2,1,0:T(8,128)}, f32[12,128,32]{2,1,0:T(8,128)}) custom-call(s32[12]{0:T(128)} %slice.50.ids_ref, s32[16]{0:T(128)} %dynamic_slice.15.count_ref, bf16[16,512,128]{2,1,0:T(8,128)(2,1)} %bitcast.30, bf16[16,512,128]{2,1,0:T(8,128)(2,1)} %bitcast.36, bf16[16,128,8]{2,1,0:T(8,128)(2,1)} %copy.30.g_ref, ...), custom_call_target="tpu_custom_call" | custom-call | flops 12079595520 | bytes 12582912 | tf_op jit(solution)/shard_map/prepare/pallas_call | solution.py:251
  92.4 11.8 %advance.4 = (bf16[16,1024,128]{2,1,0:T(8,128)(2,1)}, s32[4,520,128]{2,1,0:T(8,128)}) custom-call(s32[4]{0:T(128)} %get-tuple-element.34.ids_ref, s32[4]{0:T(128)} %get-tuple-element.38.parents_ref, s32[16]{0:T(128)} %dynamic_slice.15.count_ref, s32[1]{0:T(128)} %bitcast.15.place_ref, bf16[16,512,128]{2,1,0:T(8,128)(2,1)} %bitcast.31, ...), custom_call_target="tpu_custom_call" | custom-call | flops 1610612736 | bytes 10485760 | tf_op jit(solution)/shard_map/advance/pallas_call | solution.py:364
  104.2 11.8 %advance.5 = (bf16[16,1024,128]{2,1,0:T(8,128)(2,1)}, s32[4,520,128]{2,1,0:T(8,128)}) custom-call(s32[4]{0:T(128)} %get-tuple-element.35.ids_ref, s32[4]{0:T(128)} %get-tuple-element.39.parents_ref, s32[16]{0:T(128)} %dynamic_slice.15.count_ref, s32[1]{0:T(128)} %bitcast.13.place_ref, ...), custom_call_target="tpu_custom_call", output_to_operand_aliasing={{0}: (12, {})} | custom-call | flops 1610612736 | bytes 10485760 | tf_op jit(solution)/shard_map/advance/pallas_call | solution.py:364
  116.0 1.6 collective-permute-start.1
  117.5 2.7 %collective-permute-start.2 = (s32[4,520,128]{2,1,0:T(8,128)}, s32[4,520,128]{2,1,0:T(8,128)S(1)}, u32[]{:S(2)}, u32[]{:S(2)}) collective-permute-start(s32[4,520,128]{2,1,0:T(8,128)} %get-tuple-element.30), channel_id=1, source_target_pairs={{0,8},{4,12},{8,0},{12,4},{1,9},{5,13},{9,1},{13,5},{2,10},{6,14},... | collective-permute-start | bytes 3194888 | tf_op jit(solution)/shard_map/ppermute | solution.py:434
  120.3 11.8 %advance.6 = (bf16[16,1024,128]{2,1,0:T(8,128)(2,1)}, s32[4,520,128]{2,1,0:T(8,128)}) custom-call(s32[4]{0:T(128)} %get-tuple-element.36.ids_ref, s32[4]{0:T(128)} %get-tuple-element.40.parents_ref, s32[16]{0:T(128)} %dynamic_slice.15.count_ref, s32[1]{0:T(128)} %bitcast.7.place_ref, ...), custom_call_target="tpu_custom_call", output_to_operand_aliasing={{0}: (12, {})} | custom-call | flops 1610612736 | bytes 10485760 | tf_op jit(solution)/shard_map/advance/pallas_call | solution.py:364
  132.1 0.1 collective-permute-start
  132.2 26.6 %prepare.3 = (f32[4,8,128,128]{3,2,1,0:T(8,128)}, f32[4,8,128,128]{3,2,1,0:T(8,128)}, f32[4,128,32]{2,1,0:T(8,128)}) custom-call(s32[4]{0:T(128)} %get-tuple-element.23.ids_ref, s32[16]{0:T(128)} %dynamic_slice.15.count_ref, bf16[16,512,128]{2,1,0:T(8,128)(2,1)} %bitcast.34, bf16[16,512,128]{2,1,0:T(8,128)(2,1)} %bitcast.40, ...), custom_call_target="tpu_custom_call" | custom-call | flops 4026531840 | bytes 4194304 | tf_op jit(solution)/shard_map/prepare/pallas_call | solution.py:251
  158.7 11.7 %advance.7 = (bf16[16,1024,128]{2,1,0:T(8,128)(2,1)}, f32[16,8,128,128]{3,2,1,0:T(8,128)}) custom-call(s32[4]{0:T(128)} %get-tuple-element.23.ids_ref, s32[4]{0:T(128)} %get-tuple-element.41.parents_ref, s32[16]{0:T(128)} %dynamic_slice.15.count_ref, s32[1]{0:T(128)} %bitcast.2.place_ref, ...), custom_call_target="tpu_custom_call", output_to_operand_aliasing={{0}: (12, {})} | custom-call | flops 1610612736 | bytes 10485760 | tf_op jit(solution)/shard_map/advance/pallas_call | solution.py:364
  170.5 38.0 %collective-permute-done.2.code_ref = s32[4,520,128]{2,1,0:T(8,128)S(1)} collective-permute-done((s32[4,520,128]{2,1,0:T(8,128)}, s32[4,520,128]{2,1,0:T(8,128)S(1)}, u32[]{:S(2)}, u32[]{:S(2)}) %collective-permute-start.2) | collective-permute-done | bytes 1064992 | tf_op jit(solution)/shard_map/ppermute | solution.py:434
  208.5 1.0 copy-done.2
  209.5 3.6 %decode.3.refs_0_ = f32[16,8,128,128]{3,2,1,0:T(8,128)} custom-call(s32[1]{0:T(128)} %bitcast.15.place_ref, s32[4,520,128]{2,1,0:T(8,128)} %copy-done.2, f32[16,8,128,128]{3,2,1,0:T(8,128)} %get-tuple-element.31.refs_0_), custom_call_target="tpu_custom_call", output_to_operand_aliasing={{}: (2, {})} | custom-call | tf_op jit(solution)/shard_map/decode/pallas_call | solution.py:305
  213.1 1.0 copy-done
  214.1 3.6 %decode.4.refs_0_ = f32[16,8,128,128]{3,2,1,0:T(8,128)} custom-call(s32[1]{0:T(128)} %bitcast.13.place_ref, s32[4,520,128]{2,1,0:T(8,128)} %copy-done, f32[16,8,128,128]{3,2,1,0:T(8,128)} %decode.3.refs_0_), custom_call_target="tpu_custom_call", output_to_operand_aliasing={{}: (2, {})} | custom-call | tf_op jit(solution)/shard_map/decode/pallas_call | solution.py:305
  217.8 1.0 copy-done.1
  218.8 3.6 %decode.5 = f32[16,8,128,128]{3,2,1,0:T(8,128)} custom-call(s32[1]{0:T(128)} %bitcast.7.place_ref, s32[4,520,128]{2,1,0:T(8,128)} %copy-done.1, f32[16,8,128,128]{3,2,1,0:T(8,128)} %decode.4.refs_0_), custom_call_target="tpu_custom_call", output_to_operand_aliasing={{}: (2, {})} | custom-call | tf_op jit(solution)/shard_map/decode/pallas_call | solution.py:305
  (26 shorter events, 0.1 us)
Async XLA Ops:
  7.2 4.1 %copy-start.8 = (s32[4]{0:T(128)S(1)}, s32[4]{0:T(128)}, u32[]{:S(2)}) copy-start(s32[4]{0:T(128)} %constant.65.clone) | copy-start | bytes 52
  7.2 3.9 %copy-start.5 = (s32[64]{0:T(128)S(1)}, s32[64]{0:T(128)}, u32[]{:S(2)}) copy-start(s32[64]{0:T(128)} %param.19) | copy-start | bytes 772
  7.2 5.5 %copy-start.3 = (bf16[16,128,4,2]{1,3,2,0:T(2,128)(2,1)S(1)}, bf16[16,128,4,2]{1,3,2,0:T(2,128)(2,1)}, u32[]{:S(2)}) copy-start(bf16[16,128,4,2]{1,3,2,0:T(2,128)(2,1)} %param.15) | copy-start | bytes 98308
  7.2 6.5 %copy-start.4 = (bf16[16,128,4,2]{1,3,2,0:T(2,128)(2,1)S(1)}, bf16[16,128,4,2]{1,3,2,0:T(2,128)(2,1)}, u32[]{:S(2)}) copy-start(bf16[16,128,4,2]{1,3,2,0:T(2,128)(2,1)} %param.16) | copy-start | bytes 98308
  7.2 7.6 %copy-start.9 = (s32[64]{0:T(128)S(1)}, s32[64]{0:T(128)}, u32[]{:S(2)}) copy-start(s32[64]{0:T(128)} %param.22) | copy-start | bytes 772
  7.2 8.2 %copy-start.6 = (s32[64]{0:T(128)S(1)}, s32[64]{0:T(128)}, u32[]{:S(2)}) copy-start(s32[64]{0:T(128)} %param.21) | copy-start | bytes 772
  7.2 8.2 %copy-start.7 = (s32[64]{0:T(128)S(1)}, s32[64]{0:T(128)}, u32[]{:S(2)}) copy-start(s32[64]{0:T(128)} %param.20) | copy-start | bytes 772
  7.2 85.1 %all-gather.2.cloned.1.call-start = ((), (), s32[]{:S(2)}) async-start(), calls=%async_computation | async-start | bytes 5324800 | tf_op jit(solution)/shard_map/all_gather | solution.py:400
  116.0 97.2 %collective-permute-start.1 = (s32[4,520,128]{2,1,0:T(8,128)}, s32[4,520,128]{2,1,0:T(8,128)S(1)}, u32[]{:S(2)}, u32[]{:S(2)}) collective-permute-start(s32[4,520,128]{2,1,0:T(8,128)} %get-tuple-element.29), channel_id=1, source_target_pairs={{0,4},{4,8},{8,12},{12,0},{1,5},{5,9},{9,13},{13,1},{2,6},{6,10},{... | collective-permute-start | bytes 3194888 | tf_op jit(solution)/shard_map/ppermute | solution.py:434
  117.5 91.0 %collective-permute-start.2 = (s32[4,520,128]{2,1,0:T(8,128)}, s32[4,520,128]{2,1,0:T(8,128)S(1)}, u32[]{:S(2)}, u32[]{:S(2)}) collective-permute-start(s32[4,520,128]{2,1,0:T(8,128)} %get-tuple-element.30), channel_id=1, source_target_pairs={{0,8},{4,12},{8,0},{12,4},{1,9},{5,13},{9,1},{13,5},{2,10},{6,14},... | collective-permute-start | bytes 3194888 | tf_op jit(solution)/shard_map/ppermute | solution.py:434
  132.1 85.7 %collective-permute-start = (s32[4,520,128]{2,1,0:T(8,128)}, s32[4,520,128]{2,1,0:T(8,128)S(1)}, u32[]{:S(2)}, u32[]{:S(2)}) collective-permute-start(s32[4,520,128]{2,1,0:T(8,128)} %get-tuple-element.22), channel_id=1, source_target_pairs={{0,12},{4,0},{8,4},{12,8},{1,13},{5,1},{9,5},{13,9},{2,14},{6,2},{... | collective-permute-start | bytes 3194888 | tf_op jit(solution)/shard_map/ppermute | solution.py:434
  208.5 1.0 copy-start.2
  213.1 1.0 copy-start
  217.8 1.0 copy-start.1
Sparse Core Ops, SparseCore 0:
  11.2 80.6 all-gather.1

commit v3 on v2

--- a/solution.py
+++ b/solution.py
@@ -152,30 +152,28 @@
     while size < length:
         levels.append((size, range(size, length, 2 * size)))
         size *= 2
-    for h in range(value_heads):
+    heads = range(value_heads)
+    for h in heads:
         blocks = [jnp.where(block_masks[p], inverses[h], 0.0) for p in range(parts)]
-        result = jnp.concatenate(blocks, axis=0)
-        for size, starts in levels:
+        t_ref[0, h] = jnp.concatenate(blocks, axis=0)
+    for size, starts in levels:
+        columns = lax.broadcasted_iota(jnp.int32, (size, length), 1) // size
+        empty = jnp.zeros((size, length), F32)
+        steps = []
+        for h in heads:
             lower = [
-                jnp.where(
-                    lax.broadcasted_iota(jnp.int32, (size, length), 1) // size == start // size - 1,
-                    a_rows[h, start:start + size, :],
-                    0.0,
-                )
+                jnp.where(columns == start // size - 1, a_rows[h, start:start + size, :], 0.0)
                 for start in starts
             ]
-            step = dot3(jnp.concatenate(lower, axis=0), result)
-            empty = jnp.zeros((size, length), F32)
+            steps.append(dot3(jnp.concatenate(lower, axis=0), t_ref[0, h]))
+        for h in heads:
             spread = []
             for n in range(len(starts)):
-                spread += [empty, step[n * size:(n + 1) * size]]
-            odd = jnp.concatenate([result[start:start + size] for start in starts], axis=0)
+                spread += [empty, steps[h][n * size:(n + 1) * size]]
+            odd = jnp.concatenate([t_ref[0, h, start:start + size, :] for start in starts], axis=0)
             odd = odd - dot3(odd, jnp.concatenate(spread, axis=0))
-            joint = []
             for n, start in enumerate(starts):
-                joint += [result[start - size:start], odd[n * size:(n + 1) * size]]
-            result = jnp.concatenate(joint, axis=0)
-        t_ref[0, h] = result
+                t_ref[0, h, start:start + size, :] = odd[n * size:(n + 1) * size]
     units = jnp.concatenate(unit_cols, axis=1)
     growth = jnp.exp(g_col)
     rest = jnp.exp(g_col[length - 1:length, :] - g_col) * units
@@ -200,41 +198,42 @@
     aux = aux_ref[0]
     gain = gain_ref[...].astype(F32)
     alive = lax.broadcasted_iota(jnp.int32, (length, width), 0) < live
+    columns = lambda n, h: aux[:, n * value_heads + h:n * value_heads + h + 1]
+    half = lambda pair, r: pair[:, r * width:(r + 1) * width]
+    key_parts, applied = [], []
     for m in range(key_heads):
         q = q_rows[pl.ds(m, length, stride=key_heads), :].astype(BF16)
         k = k_rows[pl.ds(m, length, stride=key_heads), :].astype(BF16)
-        states = load_pair(s_ref, scales, m, key_dim)
-        s = jnp.concatenate(states, axis=1)
-        s_high, s_low = split(s)
+        s_high, s_low = split(jnp.concatenate(load_pair(s_ref, scales, m, key_dim), axis=1))
         kq = jnp.concatenate([k, q], axis=0)
-        applied = dot(jnp.concatenate([kq, kq], axis=1), jnp.concatenate([s_high, s_low], axis=0))
-        updates = []
-        for r in range(2):
-            h = 2 * m + r
-            growth = aux[:, h:h + 1]
-            rate = aux[:, value_heads + h:value_heads + h + 1]
-            scale = aux[:, 2 * value_heads + h:2 * value_heads + h + 1]
-            rest = aux[:, 3 * value_heads + h:3 * value_heads + h + 1]
-            v = v_rows[pl.ds(h, length, stride=value_heads), :]
-            right = rate * v - scale * applied[:length, r * width:(r + 1) * width]
-            fixed = dot3(t_ref[0, h], right)
-            out = growth * applied[length:, r * width:(r + 1) * width] + dot3(m_ref[0, h], fixed)
-            mean_square = jnp.mean(out * out, axis=1, keepdims=True)
-            normed = out * lax.rsqrt(mean_square + norm_epsilon) * gain
-            o_rows[pl.ds(h, length, stride=value_heads), :] = jnp.where(alive, normed, 0.0)
-            updates.append(rest * fixed)
-        update = jnp.concatenate(updates, axis=1)
+        key_parts.append(k)
+        applied.append(
+            dot(jnp.concatenate([kq, kq], axis=1), jnp.concatenate([s_high, s_low], axis=0))
+        )
+    fixed = []
+    for h in range(value_heads):
+        v = v_rows[pl.ds(h, length, stride=value_heads), :]
+        right = columns(1, h) * v - columns(2, h) * half(applied[h // 2][:length], h % 2)
+        fixed.append(dot3(t_ref[0, h], right))
+    for m in range(key_heads):
+        k = key_parts[m]
+        update = jnp.concatenate([columns(3, 2 * m + r) * fixed[2 * m + r] for r in range(2)], axis=1)
         u_high, u_low = split(update)
         added = dot_tn(jnp.concatenate([k, k], axis=0), jnp.concatenate([u_high, u_low], axis=0))
+        states = load_pair(s_ref, scales, m, key_dim)
         later = []
         for r in range(2):
-            h = 2 * m + r
-            last = aux[length - 1:length, h:h + 1]
-            later.append(last * states[r] + added[:, r * width:(r + 1) * width])
+            last = aux[length - 1:length, 2 * m + r:2 * m + r + 1]
+            later.append(last * states[r] + half(added, r))
         if coded:
             powers += store_pair(state_ref, m, later)
         else:
             state_ref[0, 2 * m], state_ref[0, 2 * m + 1] = later
+    for h in range(value_heads):
+        out = columns(0, h) * half(applied[h // 2][length:], h % 2) + dot3(m_ref[0, h], fixed[h])
+        mean_square = jnp.mean(out * out, axis=1, keepdims=True)
+        normed = out * lax.rsqrt(mean_square + norm_epsilon) * gain
+        o_rows[pl.ds(h, length, stride=value_heads), :] = jnp.where(alive, normed, 0.0)
     if coded:
         store_powers(state_ref, powers)
     mixed_ref[0] = o_rows[...].astype(BF16)

time: 231 us -> 227 us (0.983)
  Pallas kernels: 163 us -> 100 us
  waiting for transfers between devices: 38.1 us -> 96 us
    pallas_call x2, Pallas kernels: 101 us -> 47.8 us  [prepare(): pl.pallas_call(prepare_kernel, out_shape=(jax.ShapeDtypeStruct(square, F3...]
    all_gather x1, waiting for transfers between devices: 0.01 us -> 39.7 us  [shards(): states = lax.all_gather(codes, 'seq', axis=0, tiled=True)]
    ppermute x3, waiting for transfers between devices: 38 us -> 56.3 us  [shards(): arriving.append((place, lax.ppermute(codes, 'seq', pairs)))]
    pallas_call x4, Pallas kernels: 47.1 us -> 37.7 us  [advance(): pl.pallas_call(functools.partial(advance_kernel, coded), out_shape=(jax.S...]
  transfers between devices with their start and end apart: 4 -> 4, of which waited for: 1 -> 2; matrix products, arithmetic and copies ran while one was open for 3% -> 3% of each run, Pallas kernels for 58% -> 33%
where the time goes in v3:
time: 227 us; the launch traced here: 225 us
  Pallas kernels  100 us (44%)
  waiting for transfers between devices  96 us (42%)
  between operations  14.1 us (6%)
  local copies, waits for them, and re-layouts  9.1 us (4%)
  starting transfers between devices  4.92 us (2%)
    ppermute x3, waiting for transfers between devices, shards(): arriving.append((place, lax.ppermute(codes, 'seq', pairs)))  56.3 us
    pallas_call x2, Pallas kernels, prepare(): pl.pallas_call(prepare_kernel, out_shape=(jax.ShapeDtypeStruct(square, F3...  47.8 us
    all_gather x1, waiting for transfers between devices, shards(): states = lax.all_gather(codes, 'seq', axis=0, tiled=True)  39.7 us
    pallas_call x4, Pallas kernels, advance(): pl.pallas_call(functools.partial(advance_kernel, coded), out_shape=(jax.S...  37.7 us
    pallas_call x3, Pallas kernels, decode(): pl.pallas_call(decode_kernel, out_shape=jax.ShapeDtypeStruct(final.shape,...  10.9 us
    ppermute x3, starting transfers between devices, shards(): arriving.append((place, lax.ppermute(codes, 'seq', pairs)))  4.88 us
  transfers between devices with their start and end apart: 4, of which 2 were waited for; matrix products, arithmetic and copies ran while one was open for 3% of the time, Pallas kernels for 33%

profile of v3, /device:TPU:11, one launch (start us, length us, event | category | flops | bytes accessed | tf_op | source)
XLA Modules:
  0.0 224.7 jit_solution(8219646693745021681)
XLA Ops:
  7.3 3.8 %encode.1 = s32[4,520,128]{2,1,0:T(8,128)} custom-call(f32[4,8,128,128]{3,2,1,0:T(8,128)} %bitcast.42), custom_call_target="tpu_custom_call" | custom-call | tf_op jit(solution)/shard_map/encode/pallas_call | solution.py:290
  11.1 0.1 reshape.97
  11.2 0.1 dynamic-slice_subtract_fusion
  11.3 0.6 gather_fusion
  11.8 0.1 broadcast_select_fusion
  11.9 0.1 select_n.59
  12.0 0.1 select_n.56
  12.1 0.6 slice.50.ids_ref
  12.7 1.0 copy.30.g_ref
  13.7 1.0 copy.31.b_ref
  14.8 0.6 dynamic_slice.15.count_ref
  15.4 0.1 dynamic-slice_add_fusion
  15.5 0.7 gather_fusion.1
  16.2 0.7 fusion.2
  16.9 0.6 slice_bitcast_fusion
  17.4 34.6 %prepare.2 = (f32[12,8,128,128]{3,2,1,0:T(8,128)}, f32[12,8,128,128]{3,2,1,0:T(8,128)}, f32[12,128,32]{2,1,0:T(8,128)}) custom-call(s32[12]{0:T(128)} %slice.50.ids_ref, s32[16]{0:T(128)} %dynamic_slice.15.count_ref, bf16[16,512,128]{2,1,0:T(8,128)(2,1)} %bitcast.30, bf16[16,512,128]{2,1,0:T(8,128)(2,1)} %bitcast.36, bf16[16,128,8]{2,1,0:T(8,128)(2,1)} %copy.30.g_ref, ...), custom_call_target="tpu_custom_call" | custom-call | flops 12079595520 | bytes 12582912 | tf_op jit(solution)/shard_map/prepare/pallas_call | solution.py:250
  52.1 39.7 %all-gather.2.cloned.1.call-done.s_ref = s32[16,520,128]{2,1,0:T(8,128)} async-done(((s32[4,520,128]{2,1,0:T(8,128)}), s32[16,520,128]{2,1,0:T(8,128)}) %all-gather.2.cloned.1.call-update) | async-done | bytes 4259856 | tf_op jit(solution)/shard_map/all_gather | solution.py:399
  91.8 9.5 %advance.4 = (bf16[16,1024,128]{2,1,0:T(8,128)(2,1)}, s32[4,520,128]{2,1,0:T(8,128)}) custom-call(s32[4]{0:T(128)} %get-tuple-element.34.ids_ref, s32[4]{0:T(128)} %get-tuple-element.38.parents_ref, s32[16]{0:T(128)} %dynamic_slice.15.count_ref, s32[1]{0:T(128)} %bitcast.15.place_ref, bf16[16,512,128]{2,1,0:T(8,128)(2,1)} %bitcast.31, ...), custom_call_target="tpu_custom_call" | custom-call | flops 1610612736 | bytes 10485760 | tf_op jit(solution)/shard_map/advance/pallas_call | solution.py:363
  101.2 9.5 %advance.5 = (bf16[16,1024,128]{2,1,0:T(8,128)(2,1)}, s32[4,520,128]{2,1,0:T(8,128)}) custom-call(s32[4]{0:T(128)} %get-tuple-element.35.ids_ref, s32[4]{0:T(128)} %get-tuple-element.39.parents_ref, s32[16]{0:T(128)} %dynamic_slice.15.count_ref, s32[1]{0:T(128)} %bitcast.13.place_ref, ...), custom_call_target="tpu_custom_call", output_to_operand_aliasing={{0}: (12, {})} | custom-call | flops 1610612736 | bytes 10485760 | tf_op jit(solution)/shard_map/advance/pallas_call | solution.py:363
  110.7 2.2 collective-permute-start.1
  112.9 2.6 %collective-permute-start.2 = (s32[4,520,128]{2,1,0:T(8,128)}, s32[4,520,128]{2,1,0:T(8,128)S(1)}, u32[]{:S(2)}, u32[]{:S(2)}) collective-permute-start(s32[4,520,128]{2,1,0:T(8,128)} %get-tuple-element.30), channel_id=1, source_target_pairs={{0,8},{4,12},{8,0},{12,4},{1,9},{5,13},{9,1},{13,5},{2,10},{6,14},... | collective-permute-start | bytes 3194888 | tf_op jit(solution)/shard_map/ppermute | solution.py:433
  115.5 9.5 %advance.6 = (bf16[16,1024,128]{2,1,0:T(8,128)(2,1)}, s32[4,520,128]{2,1,0:T(8,128)}) custom-call(s32[4]{0:T(128)} %get-tuple-element.36.ids_ref, s32[4]{0:T(128)} %get-tuple-element.40.parents_ref, s32[16]{0:T(128)} %dynamic_slice.15.count_ref, s32[1]{0:T(128)} %bitcast.7.place_ref, ...), custom_call_target="tpu_custom_call", output_to_operand_aliasing={{0}: (12, {})} | custom-call | flops 1610612736 | bytes 10485760 | tf_op jit(solution)/shard_map/advance/pallas_call | solution.py:363
  125.1 0.1 collective-permute-start
  125.1 13.2 %prepare.3 = (f32[4,8,128,128]{3,2,1,0:T(8,128)}, f32[4,8,128,128]{3,2,1,0:T(8,128)}, f32[4,128,32]{2,1,0:T(8,128)}) custom-call(s32[4]{0:T(128)} %get-tuple-element.23.ids_ref, s32[16]{0:T(128)} %dynamic_slice.15.count_ref, bf16[16,512,128]{2,1,0:T(8,128)(2,1)} %bitcast.34, bf16[16,512,128]{2,1,0:T(8,128)(2,1)} %bitcast.40, ...), custom_call_target="tpu_custom_call" | custom-call | flops 4026531840 | bytes 4194304 | tf_op jit(solution)/shard_map/prepare/pallas_call | solution.py:250
  138.3 9.3 %advance.7 = (bf16[16,1024,128]{2,1,0:T(8,128)(2,1)}, f32[16,8,128,128]{3,2,1,0:T(8,128)}) custom-call(s32[4]{0:T(128)} %get-tuple-element.23.ids_ref, s32[4]{0:T(128)} %get-tuple-element.41.parents_ref, s32[16]{0:T(128)} %dynamic_slice.15.count_ref, s32[1]{0:T(128)} %bitcast.2.place_ref, ...), custom_call_target="tpu_custom_call", output_to_operand_aliasing={{0}: (12, {})} | custom-call | flops 1610612736 | bytes 10485760 | tf_op jit(solution)/shard_map/advance/pallas_call | solution.py:363
  147.6 56.3 %collective-permute-done.2.code_ref = s32[4,520,128]{2,1,0:T(8,128)S(1)} collective-permute-done((s32[4,520,128]{2,1,0:T(8,128)}, s32[4,520,128]{2,1,0:T(8,128)S(1)}, u32[]{:S(2)}, u32[]{:S(2)}) %collective-permute-start.2) | collective-permute-done | bytes 1064992 | tf_op jit(solution)/shard_map/ppermute | solution.py:433
  203.9 1.0 copy-done.2
  204.9 3.6 %decode.3.refs_0_ = f32[16,8,128,128]{3,2,1,0:T(8,128)} custom-call(s32[1]{0:T(128)} %bitcast.15.place_ref, s32[4,520,128]{2,1,0:T(8,128)} %copy-done.2, f32[16,8,128,128]{3,2,1,0:T(8,128)} %get-tuple-element.31.refs_0_), custom_call_target="tpu_custom_call", output_to_operand_aliasing={{}: (2, {})} | custom-call | tf_op jit(solution)/shard_map/decode/pallas_call | solution.py:304
  208.5 1.0 copy-done
  209.5 3.6 %decode.4.refs_0_ = f32[16,8,128,128]{3,2,1,0:T(8,128)} custom-call(s32[1]{0:T(128)} %bitcast.13.place_ref, s32[4,520,128]{2,1,0:T(8,128)} %copy-done, f32[16,8,128,128]{3,2,1,0:T(8,128)} %decode.3.refs_0_), custom_call_target="tpu_custom_call", output_to_operand_aliasing={{}: (2, {})} | custom-call | tf_op jit(solution)/shard_map/decode/pallas_call | solution.py:304
  213.2 1.0 copy-done.1
  214.2 3.6 %decode.5 = f32[16,8,128,128]{3,2,1,0:T(8,128)} custom-call(s32[1]{0:T(128)} %bitcast.7.place_ref, s32[4,520,128]{2,1,0:T(8,128)} %copy-done.1, f32[16,8,128,128]{3,2,1,0:T(8,128)} %decode.4.refs_0_), custom_call_target="tpu_custom_call", output_to_operand_aliasing={{}: (2, {})} | custom-call | tf_op jit(solution)/shard_map/decode/pallas_call | solution.py:304
  (26 shorter events, 0.1 us)
Async XLA Ops:
  7.2 4.1 %copy-start.8 = (s32[4]{0:T(128)S(1)}, s32[4]{0:T(128)}, u32[]{:S(2)}) copy-start(s32[4]{0:T(128)} %constant.65.clone) | copy-start | bytes 52
  7.2 3.9 %copy-start.5 = (s32[64]{0:T(128)S(1)}, s32[64]{0:T(128)}, u32[]{:S(2)}) copy-start(s32[64]{0:T(128)} %param.19) | copy-start | bytes 772
  7.2 5.5 %copy-start.3 = (bf16[16,128,4,2]{1,3,2,0:T(2,128)(2,1)S(1)}, bf16[16,128,4,2]{1,3,2,0:T(2,128)(2,1)}, u32[]{:S(2)}) copy-start(bf16[16,128,4,2]{1,3,2,0:T(2,128)(2,1)} %param.15) | copy-start | bytes 98308
  7.2 6.5 %copy-start.4 = (bf16[16,128,4,2]{1,3,2,0:T(2,128)(2,1)S(1)}, bf16[16,128,4,2]{1,3,2,0:T(2,128)(2,1)}, u32[]{:S(2)}) copy-start(bf16[16,128,4,2]{1,3,2,0:T(2,128)(2,1)} %param.16) | copy-start | bytes 98308
  7.2 7.6 %copy-start.9 = (s32[64]{0:T(128)S(1)}, s32[64]{0:T(128)}, u32[]{:S(2)}) copy-start(s32[64]{0:T(128)} %param.22) | copy-start | bytes 772
  7.2 8.2 %copy-start.6 = (s32[64]{0:T(128)S(1)}, s32[64]{0:T(128)}, u32[]{:S(2)}) copy-start(s32[64]{0:T(128)} %param.21) | copy-start | bytes 772
  7.2 8.2 %copy-start.7 = (s32[64]{0:T(128)S(1)}, s32[64]{0:T(128)}, u32[]{:S(2)}) copy-start(s32[64]{0:T(128)} %param.20) | copy-start | bytes 772
  7.2 84.5 %all-gather.2.cloned.1.call-start = ((), (), s32[]{:S(2)}) async-start(), calls=%async_computation | async-start | bytes 5324800 | tf_op jit(solution)/shard_map/all_gather | solution.py:399
  110.7 97.8 %collective-permute-start.1 = (s32[4,520,128]{2,1,0:T(8,128)}, s32[4,520,128]{2,1,0:T(8,128)S(1)}, u32[]{:S(2)}, u32[]{:S(2)}) collective-permute-start(s32[4,520,128]{2,1,0:T(8,128)} %get-tuple-element.29), channel_id=1, source_target_pairs={{0,4},{4,8},{8,12},{12,0},{1,5},{5,9},{9,13},{13,1},{2,6},{6,10},{... | collective-permute-start | bytes 3194888 | tf_op jit(solution)/shard_map/ppermute | solution.py:433
  112.9 91.0 %collective-permute-start.2 = (s32[4,520,128]{2,1,0:T(8,128)}, s32[4,520,128]{2,1,0:T(8,128)S(1)}, u32[]{:S(2)}, u32[]{:S(2)}) collective-permute-start(s32[4,520,128]{2,1,0:T(8,128)} %get-tuple-element.30), channel_id=1, source_target_pairs={{0,8},{4,12},{8,0},{12,4},{1,9},{5,13},{9,1},{13,5},{2,10},{6,14},... | collective-permute-start | bytes 3194888 | tf_op jit(solution)/shard_map/ppermute | solution.py:433
  125.1 88.1 %collective-permute-start = (s32[4,520,128]{2,1,0:T(8,128)}, s32[4,520,128]{2,1,0:T(8,128)S(1)}, u32[]{:S(2)}, u32[]{:S(2)}) collective-permute-start(s32[4,520,128]{2,1,0:T(8,128)} %get-tuple-element.22), channel_id=1, source_target_pairs={{0,12},{4,0},{8,4},{12,8},{1,13},{5,1},{9,5},{13,9},{2,14},{6,2},{... | collective-permute-start | bytes 3194888 | tf_op jit(solution)/shard_map/ppermute | solution.py:433
  203.9 1.0 copy-start.2
  208.5 1.0 copy-start
  213.2 1.0 copy-start.1
Sparse Core Ops, SparseCore 0:
  11.2 80.5 all-gather.1

commit v4 on v3

--- a/solution.py
+++ b/solution.py
@@ -84,13 +84,16 @@
     store_powers(code_ref, powers)
 
 
-def decode_kernel(place_ref, code_ref, *refs):
+def decode_kernel(chunks, steps, place_ref, *refs):
     del place_ref
     state_ref = refs[-1]
     heads, rows = state_ref.shape[1:3]
-    scales = load_scales(code_ref)
-    for m in range(heads // 2):
-        state_ref[0, 2 * m], state_ref[0, 2 * m + 1] = load_pair(code_ref, scales, m, rows)
+    for c in range(chunks):
+        @pl.when(lax.div(pl.program_id(0), steps) == c)
+        def _(code_ref=refs[c]):
+            scales = load_scales(code_ref)
+            for m in range(heads // 2):
+                state_ref[0, 2 * m], state_ref[0, 2 * m + 1] = load_pair(code_ref, scales, m, rows)
 
 
 def prepare_kernel(ids_ref, count_ref, q_ref, k_ref, g_ref, b_ref, t_ref, m_ref, aux_ref,
@@ -276,9 +279,9 @@
         ),
         compiler_params=pltpu.CompilerParams(vmem_limit_bytes=VMEM_BYTES),
         cost_estimate=pl.CostEstimate(
-            flops=work * 30 * 2 * length**3,
-            bytes_accessed=work * 2 * 4 * length * length,
-            transcendentals=work * length * length,
+            flops=work * 2 * length**2,
+            bytes_accessed=work * length,
+            transcendentals=work,
         ),
         name="prepare",
     )(ids, counts, queries, keys, decay, rate)
@@ -298,27 +301,30 @@
     )(states)
 
 
-def decode(place, codes, final):
-    count, rows, width = codes.shape
+def decode(places, codes, final):
+    chunks = len(codes)
+    count, rows, width = codes[0].shape
     heads, key_dim = final.shape[1:3]
+    chunk = lambda c: pl.BlockSpec(
+        (1, rows, width),
+        lambda i, place: (jnp.minimum(jnp.maximum(i - c * count, 0), count - 1), 0, 0),
+    )
     return pl.pallas_call(
-        decode_kernel,
+        functools.partial(decode_kernel, chunks, count),
         out_shape=jax.ShapeDtypeStruct(final.shape, final.dtype),
         grid_spec=pltpu.PrefetchScalarGridSpec(
             num_scalar_prefetch=1,
-            grid=(count,),
-            in_specs=[
-                pl.BlockSpec((1, rows, width), lambda i, place: (i, 0, 0)),
-                pl.BlockSpec(memory_space=pl.ANY),
-            ],
+            grid=(chunks * count,),
+            in_specs=[chunk(c) for c in range(chunks)] + [pl.BlockSpec(memory_space=pl.ANY)],
             out_specs=pl.BlockSpec(
-                (1, heads, key_dim, width), lambda i, place: (place[0] + i, 0, 0, 0)
+                (1, heads, key_dim, width),
+                lambda i, place: (place[lax.div(i, count)] + lax.rem(i, count), 0, 0, 0),
             ),
         ),
-        input_output_aliases={2: 0},
+        input_output_aliases={1 + chunks: 0},
         compiler_params=pltpu.CompilerParams(vmem_limit_bytes=VMEM_BYTES),
         name="decode",
-    )(place, codes, final)
+    )(places, *codes, final)
 
 
 def advance(ids, parents, counts, place, first, queries, keys, values, inverse, mixing, aux, gain,
@@ -378,9 +384,9 @@
         input_output_aliases=aliases,
         compiler_params=pltpu.CompilerParams(vmem_limit_bytes=VMEM_BYTES),
         cost_estimate=pl.CostEstimate(
-            flops=work * 12 * 2 * length**3,
-            bytes_accessed=work * 5 * 4 * length * length,
-            transcendentals=work * length,
+            flops=work * 2 * length**2,
+            bytes_accessed=work * length,
+            transcendentals=work,
         ),
         name="advance",
     )(*operands)
@@ -432,8 +438,10 @@
             pairs = [(d, (d + shift) % seq_count) for d in range(seq_count)]
             arriving.append((place, lax.ppermute(codes, "seq", pairs)))
     final = codes
-    for place, codes in arriving:
-        final = decode(place, codes, final)
+    for group in (arriving[:1], arriving[1:]):
+        if group:
+            places, codes = zip(*group)
+            final = decode(jnp.concatenate(places), codes, final)
     return (
         mixed.reshape(values.shape),
         final.reshape((expansions,) + parent_cache.shape[1:]),

time: 227 us -> 213 us (0.938)
  waiting for transfers between devices: 96 us -> 84 us
    ppermute x3, waiting for transfers between devices: 56.3 us -> 44.2 us  [shards(): arriving.append((place, lax.ppermute(codes, 'seq', pairs)))]
    pallas_call x3 -> x2, Pallas kernels: 10.9 us -> 10.5 us  [decode(): pl.pallas_call(functools.partial(decode_kernel, chunks, count), out_shape...]
  transfers between devices with their start and end apart: 4 -> 4, of which waited for: 2 -> 3; matrix products, arithmetic and copies ran while one was open for 3% -> 3% of each run, Pallas kernels for 33% -> 38%
where the time goes in v4:
time: 213 us; the launch traced here: 212 us
  Pallas kernels  99.9 us (47%)
  waiting for transfers between devices  84 us (39%)
  between operations  14.1 us (7%)
  local copies, waits for them, and re-layouts  8.9 us (4%)
  starting transfers between devices  4.19 us (2%)
    pallas_call x2, Pallas kernels, prepare(): pl.pallas_call(prepare_kernel, out_shape=(jax.ShapeDtypeStruct(square, F3...  47.8 us
    ppermute x3, waiting for transfers between devices, shards(): arriving.append((place, lax.ppermute(codes, 'seq', pairs)))  44.2 us
    all_gather x1, waiting for transfers between devices, shards(): states = lax.all_gather(codes, 'seq', axis=0, tiled=True)  39.8 us
    pallas_call x4, Pallas kernels, advance(): pl.pallas_call(functools.partial(advance_kernel, coded), out_shape=(jax.S...  37.7 us
    pallas_call x2, Pallas kernels, decode(): pl.pallas_call(functools.partial(decode_kernel, chunks, count), out_shape...  10.5 us
  transfers between devices with their start and end apart: 4, of which 3 were waited for; matrix products, arithmetic and copies ran while one was open for 3% of the time, Pallas kernels for 38%

profile of v4, /device:TPU:11, one launch (start us, length us, event | category | flops | bytes accessed | tf_op | source)
XLA Modules:
  0.0 212.0 jit_solution(1359568232745736570)
XLA Ops:
  7.3 3.8 %encode.1 = s32[4,520,128]{2,1,0:T(8,128)} custom-call(f32[4,8,128,128]{3,2,1,0:T(8,128)} %bitcast.42), custom_call_target="tpu_custom_call" | custom-call | tf_op jit(solution)/shard_map/encode/pallas_call | solution.py:293
  11.1 0.1 reshape.97
  11.2 0.1 dynamic-slice_subtract_fusion
  11.3 0.6 gather_fusion
  11.9 0.1 select_n.59
  12.0 0.1 select_n.56
  12.1 0.6 slice.50.ids_ref
  12.7 1.0 copy.29.g_ref
  13.7 1.0 copy.30.b_ref
  14.7 0.6 dynamic_slice.15.count_ref
  15.3 0.1 dynamic-slice_add_fusion
  15.4 0.7 gather_fusion.1
  16.0 34.7 %prepare.2 = (f32[12,8,128,128]{3,2,1,0:T(8,128)}, f32[12,8,128,128]{3,2,1,0:T(8,128)}, f32[12,128,32]{2,1,0:T(8,128)}) custom-call(s32[12]{0:T(128)} %slice.50.ids_ref, s32[16]{0:T(128)} %dynamic_slice.15.count_ref, bf16[16,512,128]{2,1,0:T(8,128)(2,1)} %bitcast.24, bf16[16,512,128]{2,1,0:T(8,128)(2,1)} %bitcast.30, bf16[16,128,8]{2,1,0:T(8,128)(2,1)} %copy.29.g_ref, ...), custom_call_target="tpu_custom_call" | custom-call | flops 3145728 | bytes 12288 | tf_op jit(solution)/shard_map/prepare/pallas_call | solution.py:253
  50.7 0.7 fusion.2
  51.4 0.6 slice_bitcast_fusion
  52.0 39.8 %all-gather.2.cloned.1.call-done.s_ref = s32[16,520,128]{2,1,0:T(8,128)} async-done(((s32[4,520,128]{2,1,0:T(8,128)}), s32[16,520,128]{2,1,0:T(8,128)}) %all-gather.2.cloned.1.call-update) | async-done | bytes 4259856 | tf_op jit(solution)/shard_map/all_gather | solution.py:405
  91.8 9.5 %advance.4 = (bf16[16,1024,128]{2,1,0:T(8,128)(2,1)}, s32[4,520,128]{2,1,0:T(8,128)}) custom-call(s32[4]{0:T(128)} %get-tuple-element.34.ids_ref, s32[4]{0:T(128)} %get-tuple-element.38.parents_ref, s32[16]{0:T(128)} %dynamic_slice.15.count_ref, s32[1]{0:T(128)} %bitcast.15.place_ref, bf16[16,512,128]{2,1,0:T(8,128)(2,1)} %bitcast.25, ...), custom_call_target="tpu_custom_call" | custom-call | flops 1048576 | bytes 4096 | tf_op jit(solution)/shard_map/advance/pallas_call | solution.py:369
  101.3 2.3 %collective-permute-start.2 = (s32[4,520,128]{2,1,0:T(8,128)}, s32[4,520,128]{2,1,0:T(8,128)S(1)}, u32[]{:S(2)}, u32[]{:S(2)}) collective-permute-start(s32[4,520,128]{2,1,0:T(8,128)} %get-tuple-element.30), channel_id=1, source_target_pairs={{0,8},{4,12},{8,0},{12,4},{1,9},{5,13},{9,1},{13,5},{2,10},{6,14},... | collective-permute-start | bytes 3194888 | tf_op jit(solution)/shard_map/ppermute | solution.py:439
  103.6 9.5 %advance.5 = (bf16[16,1024,128]{2,1,0:T(8,128)(2,1)}, s32[4,520,128]{2,1,0:T(8,128)}) custom-call(s32[4]{0:T(128)} %get-tuple-element.35.ids_ref, s32[4]{0:T(128)} %get-tuple-element.39.parents_ref, s32[16]{0:T(128)} %dynamic_slice.15.count_ref, s32[1]{0:T(128)} %bitcast.13.place_ref, ...), custom_call_target="tpu_custom_call", output_to_operand_aliasing={{0}: (12, {})} | custom-call | flops 1048576 | bytes 4096 | tf_op jit(solution)/shard_map/advance/pallas_call | solution.py:369
  113.1 9.5 %advance.6 = (bf16[16,1024,128]{2,1,0:T(8,128)(2,1)}, s32[4,520,128]{2,1,0:T(8,128)}) custom-call(s32[4]{0:T(128)} %get-tuple-element.36.ids_ref, s32[4]{0:T(128)} %get-tuple-element.40.parents_ref, s32[16]{0:T(128)} %dynamic_slice.15.count_ref, s32[1]{0:T(128)} %bitcast.7.place_ref, ...), custom_call_target="tpu_custom_call", output_to_operand_aliasing={{0}: (12, {})} | custom-call | flops 1048576 | bytes 4096 | tf_op jit(solution)/shard_map/advance/pallas_call | solution.py:369
  122.6 1.1 collective-permute-start.1
  123.7 0.8 collective-permute-start
  124.4 0.6 pad_add_fusion.place_ref
  125.1 13.2 %prepare.3 = (f32[4,8,128,128]{3,2,1,0:T(8,128)}, f32[4,8,128,128]{3,2,1,0:T(8,128)}, f32[4,128,32]{2,1,0:T(8,128)}) custom-call(s32[4]{0:T(128)} %get-tuple-element.23.ids_ref, s32[16]{0:T(128)} %dynamic_slice.15.count_ref, bf16[16,512,128]{2,1,0:T(8,128)(2,1)} %bitcast.28, bf16[16,512,128]{2,1,0:T(8,128)(2,1)} %bitcast.34, ...), custom_call_target="tpu_custom_call" | custom-call | flops 1048576 | bytes 4096 | tf_op jit(solution)/shard_map/prepare/pallas_call | solution.py:253
  138.2 9.3 %advance.7 = (bf16[16,1024,128]{2,1,0:T(8,128)(2,1)}, f32[16,8,128,128]{3,2,1,0:T(8,128)}) custom-call(s32[4]{0:T(128)} %get-tuple-element.23.ids_ref, s32[4]{0:T(128)} %get-tuple-element.41.parents_ref, s32[16]{0:T(128)} %dynamic_slice.15.count_ref, s32[1]{0:T(128)} %bitcast.2.place_ref, ...), custom_call_target="tpu_custom_call", output_to_operand_aliasing={{0}: (12, {})} | custom-call | flops 1048576 | bytes 4096 | tf_op jit(solution)/shard_map/advance/pallas_call | solution.py:369
  147.5 24.5 %collective-permute-done.2.refs_0_ = s32[4,520,128]{2,1,0:T(8,128)S(1)} collective-permute-done((s32[4,520,128]{2,1,0:T(8,128)}, s32[4,520,128]{2,1,0:T(8,128)S(1)}, u32[]{:S(2)}, u32[]{:S(2)}) %collective-permute-start.2) | collective-permute-done | bytes 1064992 | tf_op jit(solution)/shard_map/ppermute | solution.py:439
  172.0 1.0 copy-done
  173.0 3.6 %decode.2.refs_2_ = f32[16,8,128,128]{3,2,1,0:T(8,128)} custom-call(s32[1]{0:T(128)} %bitcast.15.place_ref, s32[4,520,128]{2,1,0:T(8,128)} %copy-done, f32[16,8,128,128]{3,2,1,0:T(8,128)} %get-tuple-element.31.refs_1_), custom_call_target="tpu_custom_call", output_to_operand_aliasing={{}: (2, {})} | custom-call | tf_op jit(solution)/shard_map/decode/pallas_call | solution.py:312
  176.7 19.6 %collective-permute-done.1.refs_1_ = s32[4,520,128]{2,1,0:T(8,128)S(1)} collective-permute-done((s32[4,520,128]{2,1,0:T(8,128)}, s32[4,520,128]{2,1,0:T(8,128)S(1)}, u32[]{:S(2)}, u32[]{:S(2)}) %collective-permute-start.1) | collective-permute-done | bytes 1064992 | tf_op jit(solution)/shard_map/ppermute | solution.py:439
  196.3 1.0 copy-done.1
  197.3 1.0 copy-done.2
  198.3 6.9 %decode.3 = f32[16,8,128,128]{3,2,1,0:T(8,128)} custom-call(s32[2]{0:T(128)} %pad_add_fusion.place_ref, s32[4,520,128]{2,1,0:T(8,128)} %copy-done.2, s32[4,520,128]{2,1,0:T(8,128)} %copy-done.1, f32[16,8,128,128]{3,2,1,0:T(8,128)} %decode.2.refs_2_), custom_call_target="tpu_custom_call", output_to_operand_aliasing={{}: (3, {})} | custom-call | tf_op jit(solution)/shard_map/decode/pallas_call | solution.py:312
  (26 shorter events, 0.2 us)
Async XLA Ops:
  7.2 84.6 %all-gather.2.cloned.1.call-start = ((), (), s32[]{:S(2)}) async-start(), calls=%async_computation | async-start | bytes 5324800 | tf_op jit(solution)/shard_map/all_gather | solution.py:405
  7.2 3.9 %copy-start.5 = (s32[64]{0:T(128)S(1)}, s32[64]{0:T(128)}, u32[]{:S(2)}) copy-start(s32[64]{0:T(128)} %param.19) | copy-start | bytes 772
  7.2 4.1 %copy-start.8 = (s32[4]{0:T(128)S(1)}, s32[4]{0:T(128)}, u32[]{:S(2)}) copy-start(s32[4]{0:T(128)} %constant.65.clone) | copy-start | bytes 52
  7.2 5.4 %copy-start.3 = (bf16[16,128,4,2]{1,3,2,0:T(2,128)(2,1)S(1)}, bf16[16,128,4,2]{1,3,2,0:T(2,128)(2,1)}, u32[]{:S(2)}) copy-start(bf16[16,128,4,2]{1,3,2,0:T(2,128)(2,1)} %param.15) | copy-start | bytes 98308
  7.2 6.5 %copy-start.4 = (bf16[16,128,4,2]{1,3,2,0:T(2,128)(2,1)S(1)}, bf16[16,128,4,2]{1,3,2,0:T(2,128)(2,1)}, u32[]{:S(2)}) copy-start(bf16[16,128,4,2]{1,3,2,0:T(2,128)(2,1)} %param.16) | copy-start | bytes 98308
  7.3 7.5 %copy-start.9 = (s32[64]{0:T(128)S(1)}, s32[64]{0:T(128)}, u32[]{:S(2)}) copy-start(s32[64]{0:T(128)} %param.22) | copy-start | bytes 772
  7.3 8.0 %copy-start.6 = (s32[64]{0:T(128)S(1)}, s32[64]{0:T(128)}, u32[]{:S(2)}) copy-start(s32[64]{0:T(128)} %param.21) | copy-start | bytes 772
  7.3 8.0 %copy-start.7 = (s32[64]{0:T(128)S(1)}, s32[64]{0:T(128)}, u32[]{:S(2)}) copy-start(s32[64]{0:T(128)} %param.20) | copy-start | bytes 772
  101.3 70.8 %collective-permute-start.2 = (s32[4,520,128]{2,1,0:T(8,128)}, s32[4,520,128]{2,1,0:T(8,128)S(1)}, u32[]{:S(2)}, u32[]{:S(2)}) collective-permute-start(s32[4,520,128]{2,1,0:T(8,128)} %get-tuple-element.30), channel_id=1, source_target_pairs={{0,8},{4,12},{8,0},{12,4},{1,9},{5,13},{9,1},{13,5},{2,10},{6,14},... | collective-permute-start | bytes 3194888 | tf_op jit(solution)/shard_map/ppermute | solution.py:439
  122.6 73.7 %collective-permute-start.1 = (s32[4,520,128]{2,1,0:T(8,128)}, s32[4,520,128]{2,1,0:T(8,128)S(1)}, u32[]{:S(2)}, u32[]{:S(2)}) collective-permute-start(s32[4,520,128]{2,1,0:T(8,128)} %get-tuple-element.22), channel_id=1, source_target_pairs={{0,12},{4,0},{8,4},{12,8},{1,13},{5,1},{9,5},{13,9},{2,14},{6,2},{... | collective-permute-start | bytes 3194888 | tf_op jit(solution)/shard_map/ppermute | solution.py:439
  123.7 72.7 %collective-permute-start = (s32[4,520,128]{2,1,0:T(8,128)}, s32[4,520,128]{2,1,0:T(8,128)S(1)}, u32[]{:S(2)}, u32[]{:S(2)}) collective-permute-start(s32[4,520,128]{2,1,0:T(8,128)} %get-tuple-element.29), channel_id=1, source_target_pairs={{0,4},{4,8},{8,12},{12,0},{1,5},{5,9},{9,13},{13,1},{2,6},{6,10},{... | collective-permute-start | bytes 3194888 | tf_op jit(solution)/shard_map/ppermute | solution.py:439
  172.0 1.0 copy-start
  196.3 1.0 copy-start.1
  197.3 1.0 copy-start.2
Sparse Core Ops, SparseCore 0:
  11.2 80.5 all-gather.1
